TPU v7x, 256 devices: a whole 4x4x8 slice. The times are simulated.
256 devices in a mesh: seq: 64 (over y, z, core), mp: 4 (over x).
Axes of the slice: x: 4, y: 4, z: 8, core: 2. Of those that a mesh axis runs over, the one named last changes fastest.
Arguments:
- query: bfloat16 [16384, 2048], P('seq', 'mp'), may hold values from -5 to 5
- key: bfloat16 [16384, 2048], P('seq', 'mp'), may hold values from -5 to 5
- value: bfloat16 [16384, 2048], P('seq', 'mp'), may hold values from -6 to 6
- feat_query: bfloat16 [16384, 256], P('seq', 'mp'), may hold values from -4 to 4
- feat_key: bfloat16 [16384, 256], P('seq', 'mp'), may hold values from -4 to 4
- log_decay: float32 [16, 16384], P('mp', 'seq'), may hold values from -0.5 to 0
- band_width: int32 [256], P('seq'), may hold values from 16 to 64, as said below
- norm_gain: float32 [2048], P('mp'), may hold values from 0.5 to 1.5
- out_weight: bfloat16 [2048, 2048], P('mp'), may hold values from -0.125 to 0.125
- grad_out: bfloat16 [16384, 2048], P(('seq', 'mp')), may hold values from -6 to 6
Outputs:
- layer_out: bfloat16 [16384, 2048], P(('seq', 'mp'))
- grad_query: bfloat16 [16384, 2048], P('seq', 'mp')
- grad_key: bfloat16 [16384, 2048], P('seq', 'mp')
- grad_value: bfloat16 [16384, 2048], P('seq', 'mp')
- grad_feat_query: bfloat16 [16384, 256], P('seq', 'mp')
- grad_feat_key: bfloat16 [16384, 256], P('seq', 'mp')
Inputs may be any that keep to these rules, and one draw needn't show every extreme that they name: `band_width`: entry b is the window width of query rows b * 64 to (b + 1) * 64 - 1; the first block of some device other than the first has width 64.
All inputs are finite; a program needn't handle non-finite values.
Results may differ from a plain program's by a relative error of at most 0.015.
Values may be sent and summed in bfloat16 or wider, within the bound.
No kernel may reach another device: no remote copies, remote signals or barrier semaphores. Data moves between devices by JAX's collectives and lax.ppermute only.
A program may use at most 128 MiB of HBM per device.

v0:
```python
import numpy as np
import ml_dtypes
import jax
import jax.numpy as jnp
from jax import lax
from jax.experimental import pallas as pl
from jax.experimental.pallas import tpu as pltpu
from jax.sharding import PartitionSpec as P

WINDOW = 64
EPS = 1e-06
NEG = -1e30
F32 = jnp.float32
BF16 = jnp.bfloat16
TOK = 256
HEADS = 4
SIZE = 128
FEAT = 16
ROWS = 256
SCALE = SIZE**-0.5

NN = (((1,), (0,)), ((), ()))
NT = (((1,), (1,)), ((), ()))
TN = (((0,), (0,)), ((), ()))


def mm(a, b, dims):
    return lax.dot_general(a, b, dims, preferred_element_type=F32)


def selectors(query_side):
    first = np.zeros((ROWS, FEAT), np.float32)
    second = np.zeros_like(first)
    weight = [1 / 32] + [1 / 16] * 7 + [1 / 32, 1 / 4]
    for a in range(FEAT):
        for r in range(10):
            first[a * 16 + r, a] = weight[r] if query_side else 1.0
            if r < 9:
                second[a * 16 + r, (a + r) % FEAT] = 1.0
    both = np.concatenate([first, second], axis=0).astype(ml_dtypes.bfloat16)
    return (both, np.ascontiguousarray(both.T))


SEL_K, SEL_K_T = selectors(False)
SEL_Q, SEL_Q_T = selectors(True)


def row_kind(shape, dim):
    return lax.broadcasted_iota(jnp.int32, shape, dim) % 16


def factors_rows(feats_t, sel, const):
    both = mm(sel, feats_t, NN)
    kind = row_kind((ROWS, 1), 0)
    left = both[:ROWS, :] + jnp.where(kind == 10, const, 0.0)
    right = both[ROWS:, :] + jnp.where((kind == 9) | (kind == 10), 1.0, 0.0)
    return (left, right)


def factors_cols(feats_t, sel_t, const):
    both = mm(feats_t, sel_t, TN)
    kind = row_kind((1, ROWS), 1)
    left = both[:, :ROWS] + jnp.where(kind == 10, const, 0.0)
    right = both[:, ROWS:] + jnp.where((kind == 9) | (kind == 10), 1.0, 0.0)
    return (left, right)


def feature_grad(grad_phi, left, right, sel_t):
    both = jnp.concatenate([grad_phi * right, grad_phi * left], axis=0)
    return mm(sel_t, both.astype(BF16), NN)


def split3(value):
    hi = value.astype(BF16)
    rest = value - hi.astype(F32)
    mid = rest.astype(BF16)
    low = (rest - mid.astype(F32)).astype(BF16)
    return (hi, mid, low)


def with_total(state, total):
    kind = row_kind((ROWS, 1), 0)
    hi, mid, low = split3(total)
    state = jnp.where(kind == 11, hi.astype(F32), state)
    state = jnp.where(kind == 12, mid.astype(F32), state)
    return jnp.where(kind == 13, low.astype(F32), state)


def local_state_kernel(
    feat_t, value, key_tail, decay, sel, state_out, cum_out, cum_row_out, edge_out
):
    edge_out[:WINDOW, :] = key_tail[...]
    edge_out[WINDOW:, :] = value[TOK - WINDOW :, :]
    tri = (
        lax.broadcasted_iota(jnp.int32, (TOK, TOK), 0)
        >= lax.broadcasted_iota(jnp.int32, (TOK, TOK), 1)
    ).astype(F32).astype(BF16)
    parts = split3(decay[...])
    cum_row_out[:, 0, :] = sum(mm(p, tri, NT) for p in parts)
    for h in range(HEADS):
        cum = sum(
            mm(tri, jnp.broadcast_to(p[h : h + 1, :], (SIZE, TOK)), NT) for p in parts
        )
        cum_out[:, h * SIZE : (h + 1) * SIZE] = cum
        total = cum[TOK - 1 : TOK, :]
        rows = slice(h * ROWS, (h + 1) * ROWS)
        left, right = factors_rows(feat_t[h * FEAT : (h + 1) * FEAT, :], sel[...], 1.0)
        phi = (left * right).astype(BF16)
        scaled = value[:, h * SIZE : (h + 1) * SIZE].astype(F32) * jnp.exp(total - cum)
        state = mm(phi, scaled.astype(BF16), NN)
        state_out[rows, :] = with_total(state, total).astype(BF16)


def chain_kernel(reverse, arrived, before_out):
    count = arrived.shape[0]
    carry = jnp.zeros((16, SIZE), F32)
    order = range(count)
    for j in reversed(order) if reverse else order:
        before_out[j] = carry.astype(BF16)
        piece = arrived[j].astype(F32)
        total = piece[11:12] + piece[12:13] + piece[13:14]
        carry = carry * jnp.exp(total) + piece


def intra_weights(fq_t, fk_t, cum, cum_row):
    inner = mm(fq_t, fk_t, TN) * FEAT**-0.5
    span = jnp.concatenate([cum, cum], axis=1) - cum_row
    causal = lax.broadcasted_iota(jnp.int32, (TOK, TOK), 0) >= lax.broadcasted_iota(
        jnp.int32, (TOK, TOK), 1
    )
    fade = jnp.where(causal, jnp.exp(jnp.minimum(span, 0.0)), 0.0)
    return (inner, fade, (1.0 + inner + 0.5 * inner * inner) * fade)


def block_pair(before, array, b):
    if b == 0:
        return jnp.concatenate([before, array[:WINDOW, :]], axis=0)
    return array[(b - 1) * WINDOW : (b + 1) * WINDOW, :]


def intra_kernel(fq_t, fk_t, value, cum, cum_row, sel, sel_t, local_out, phi_out, phit_out):
    _, _, weights = intra_weights(fq_t[...], fk_t[...], cum[...], cum_row[0])
    local_out[...] = mm(weights.astype(BF16), value[...], NN)
    left, right = factors_cols(fq_t[...], sel_t[...], 1 / 16)
    phi_out[...] = (left * right).astype(BF16)
    left, right = factors_rows(fq_t[...], sel[...], 1 / 16)
    phit_out[...] = (left * right).astype(BF16)


def window_kernel(band, query, key, value, before, attended_out, probs_out):
    row = lax.broadcasted_iota(jnp.int32, (WINDOW, 2 * WINDOW), 0)
    col = lax.broadcasted_iota(jnp.int32, (WINDOW, 2 * WINDOW), 1)
    back = WINDOW + row - col
    for b in range(TOK // WINDOW):
        here = slice(b * WINDOW, (b + 1) * WINDOW)
        allowed = (back >= 0) & (back < band[b])
        if b == 0:
            allowed = allowed & (col >= band[TOK // WINDOW])
        for h in range(query.shape[1] // SIZE):
            cols = slice(h * SIZE, (h + 1) * SIZE)
            keys = block_pair(before[:WINDOW, cols], key.at[:, cols], b)
            values = block_pair(before[WINDOW:, cols], value.at[:, cols], b)
            scores = mm(query[here, cols], keys, NT) * SCALE
            scores = jnp.where(allowed, scores, NEG)
            expo = jnp.exp(scores - jnp.max(scores, axis=-1, keepdims=True))
            probs = expo / jnp.sum(expo, axis=-1, keepdims=True)
            probs16 = probs.astype(BF16)
            probs_out[here, cols] = probs16
            attended_out[here, cols] = mm(probs16, values, NN)


def window_grad_kernel(
    query, key, value, before, probs, grad_rows, weight, grad_out, gq_out, gk_out, gv_out, edge_out
):
    grad = mm(grad_rows[...], weight[...], NT)
    grad_out[...] = grad
    grad16 = grad.astype(BF16)
    for h in range(query.shape[1] // SIZE):
        cols = slice(h * SIZE, (h + 1) * SIZE)
        key_parts = []
        value_parts = []
        for b in range(TOK // WINDOW):
            here = slice(b * WINDOW, (b + 1) * WINDOW)
            keys = block_pair(before[:WINDOW, cols], key.at[:, cols], b)
            values = block_pair(before[WINDOW:, cols], value.at[:, cols], b)
            probs16 = probs[here, cols]
            probs32 = probs16.astype(F32)
            grad_here = grad16[here, cols]
            grad_probs = mm(grad_here, values, NT).astype(BF16).astype(F32)
            along = jnp.sum(probs32 * grad_probs, axis=-1, keepdims=True)
            grad_scores = (probs32 * (grad_probs - along) * SCALE).astype(BF16)
            gq_out[here, cols] = mm(grad_scores, keys, NN).astype(BF16)
            key_parts.append(mm(grad_scores, query[here, cols], TN).astype(BF16))
            value_parts.append(mm(probs16, grad_here, TN).astype(BF16))
        for place, parts, out in ((0, key_parts, gk_out), (WINDOW, value_parts, gv_out)):
            edge_out[place : place + WINDOW, cols] = parts[0][:WINDOW, :]
            for b in range(TOK // WINDOW):
                own = parts[b][WINDOW:, :]
                if b + 1 < TOK // WINDOW:
                    own = own + parts[b + 1][:WINDOW, :]
                out[b * WINDOW : (b + 1) * WINDOW, cols] = own


def mix_kernel(
    state, phi, phit, local, attended, grad, cum, gain, mixed_out, grad_linear_out, grad_state_out
):
    cum = cum[...]
    fade = jnp.exp(cum)
    linear = local[...] + fade * mm(phi[...], state[...], NN)
    scale = lax.rsqrt(jnp.mean(linear * linear, axis=-1, keepdims=True) + EPS)
    mixed_out[...] = (attended[...] + linear * scale * gain[...]).astype(BF16)
    scaled = grad[...] * gain[...]
    along = jnp.mean(scaled * linear, axis=-1, keepdims=True)
    grad_linear = scale * scaled - linear * (scale * scale * scale * along)
    grad_linear_out[...] = grad_linear.astype(BF16)
    grad_state = mm(phit[...], (grad_linear * fade).astype(BF16), NN)
    grad_state_out[...] = with_total(grad_state, cum[TOK - 1 : TOK, :]).astype(BF16)


def intra_grad_kernel(
    fq_t, fk_t, value, cum, cum_row, sel, sel_t, state, grad_linear, gq_out, gk_out, gv_out
):
    fq_t, fk_t, grads = (fq_t[...], fk_t[...], grad_linear[...])
    inner, fade, weights = intra_weights(fq_t, fk_t, cum[...], cum_row[0])
    gv_out[...] = mm(weights.astype(BF16), grads, TN)
    grad_inner = mm(grads, value[...], NT) * fade * (1.0 + inner) * FEAT**-0.5
    grad_inner = grad_inner.astype(BF16)
    gk_out[...] = mm(fq_t, grad_inner, NN)
    faded = (grads.astype(F32) * jnp.exp(cum[...])).astype(BF16)
    grad_phi = mm(state[...], faded, NT)
    left, right = factors_rows(fq_t, sel[...], 1 / 16)
    gq = mm(fk_t, grad_inner, NT) + feature_grad(grad_phi, left, right, sel_t[...])
    gq_out[...] = gq.astype(BF16)


def finish_kernel(
    fk_t, value, cum, sel, sel_t, suffix, gv_local, gk_local, window_key, window_value, edge,
    gk_out, gv_out, gfk_out
):
    cum = cum[...]
    fade = jnp.exp(cum[TOK - 1 : TOK, :] - cum)
    left, right = factors_cols(fk_t[...], sel_t[...], 1.0)
    carried = mm((left * right).astype(BF16), suffix[...], NN) * fade
    gv = (gv_local[...] + carried).astype(BF16)
    last = TOK - WINDOW
    gv_out[:last, :] = window_value[:last, :] + gv[:last, :]
    gv_out[last:, :] = (window_value[last:, :] + edge[WINDOW:, :]) + gv[last:, :]
    gk_out[:last, :] = window_key[:last, :]
    gk_out[last:, :] = window_key[last:, :] + edge[:WINDOW, :]
    faded = (value[...].astype(F32) * fade).astype(BF16)
    grad_phi = mm(suffix[...], faded, NT)
    left, right = factors_rows(fk_t[...], sel[...], 1.0)
    gfk_out[...] = (gk_local[...] + feature_grad(grad_phi, left, right, sel_t[...])).astype(BF16)


def shape(dims, kind):
    return jax.ShapeDtypeStruct(dims, kind)


def whole(*dims):
    return pl.BlockSpec(dims, lambda h: (0,) * len(dims))


def cols(rows, heads=1):
    return pl.BlockSpec((rows, heads * SIZE), lambda h: (0, h))


COLS = cols(TOK)
PAIR = cols(TOK, 2)
STATE = pl.BlockSpec((ROWS, SIZE), lambda h: (h, 0))
PHI = pl.BlockSpec((TOK, ROWS), lambda h: (0, h))
PHIT = pl.BlockSpec((ROWS, TOK), lambda h: (h, 0))
FEATS = pl.BlockSpec((FEAT, TOK), lambda h: (h, 0))
CROW = pl.BlockSpec((1, 1, TOK), lambda h: (h, 0, 0))
SEL = whole(2 * ROWS, FEAT)
SEL_T = whole(FEAT, 2 * ROWS)


def params(mib):
    return pltpu.CompilerParams(vmem_limit_bytes=mib << 20)


def cost(flops, moved):
    return pl.CostEstimate(flops=flops, transcendentals=0, bytes_accessed=moved)


def swap(value):
    return lax.all_to_all(value, "seq", split_axis=0, concat_axis=0, tiled=True)


def chain(arrived, reverse):
    return pl.pallas_call(
        lambda a, o: chain_kernel(reverse, a, o),
        out_shape=shape(arrived.shape, BF16),
        name="chain_back" if reverse else "chain_fwd",
        compiler_params=params(4),
        cost_estimate=cost(1 << 20, 1 << 19),
    )(arrived)


def after(value, *others):
    return lax.optimization_barrier((value, *others))


def shifted(value, ways, k):
    return lax.ppermute(value, "mp", [(i, (i + k) % ways) for i in range(ways)])


def body(
    query, key, value, feat_query, feat_key, log_decay, band_width, norm_gain, out_weight, grad_out
):
    count, width = query.shape
    peers = lax.axis_size("seq")
    place = lax.axis_index("seq")
    ways = lax.axis_size("mp")
    lane = lax.axis_index("mp")
    sel_k, sel_kt, sel_q, sel_qt = (jnp.asarray(m) for m in (SEL_K, SEL_K_T, SEL_Q, SEL_Q_T))
    wide32 = shape((count, width), F32)
    wide16 = shape((count, width), BF16)
    edge16 = shape((2 * WINDOW, width), BF16)
    states = shape((HEADS * ROWS, SIZE), BF16)
    chunks = (peers, HEADS * ROWS // peers, SIZE)
    fq_t, fk_t = (feat_query.T, feat_key.T)
    model = grad_out.shape[1]

    state, cum, cum_row, edge = pl.pallas_call(
        local_state_kernel,
        grid=(1,),
        in_specs=[
            whole(HEADS * FEAT, TOK),
            whole(TOK, width),
            pl.BlockSpec((WINDOW, width), lambda h: (TOK // WINDOW - 1, 0)),
            whole(HEADS, TOK),
            SEL,
        ],
        out_specs=[
            whole(HEADS * ROWS, SIZE),
            whole(TOK, width),
            whole(HEADS, 1, TOK),
            whole(2 * WINDOW, width),
        ],
        out_shape=[states, wide32, shape((HEADS, 1, TOK), F32), edge16],
        compiler_params=params(12),
        name="local_state",
    )(fk_t, value, key, log_decay, sel_k)

    arrived = swap(state.reshape(chunks))

    before = lax.ppermute(edge, "seq", [(i, i + 1) for i in range(peers - 1)])
    grad_pieces = [grad_out] + [shifted(grad_out, ways, k) for k in range(1, ways)]

    local, phi, phit = pl.pallas_call(
        intra_kernel,
        grid=(HEADS,),
        in_specs=[FEATS, FEATS, COLS, COLS, CROW, SEL, SEL_T],
        out_specs=[COLS, PHI, PHIT],
        out_shape=[wide32, shape((TOK, HEADS * ROWS), BF16), shape((HEADS * ROWS, TOK), BF16)],
        compiler_params=params(8),
        name="intra",
    )(fq_t, fk_t, value, cum, cum_row, sel_q, sel_qt)

    first_col = jnp.where(place == 0, WINDOW, 0).astype(jnp.int32)
    band = jnp.concatenate([band_width, first_col[None]])
    attended, probs = pl.pallas_call(
        window_kernel,
        grid=(HEADS // 2,),
        in_specs=[
            pl.BlockSpec(memory_space=pltpu.SMEM),
            PAIR,
            PAIR,
            PAIR,
            cols(2 * WINDOW, 2),
        ],
        out_specs=[PAIR, PAIR],
        out_shape=[wide32, wide16],
        compiler_params=params(8),
        name="window",
    )(band, query, key, value, before)

    arrived, attended, probs, local, phi, phit = after(
        arrived, attended, probs, local, phi, phit
    )
    prefix = swap(chain(arrived, False))

    grad_rows = jnp.zeros((ways, count // ways, model), BF16)
    for k, piece in enumerate(grad_pieces):
        grad_rows = lax.dynamic_update_slice(grad_rows, piece[None], ((lane - k) % ways, 0, 0))
    grad_rows = grad_rows.reshape(count, model)

    grad, grad_query, win_key, win_value, edge_grad = pl.pallas_call(
        window_grad_kernel,
        grid=(HEADS // 2,),
        in_specs=[
            PAIR,
            PAIR,
            PAIR,
            cols(2 * WINDOW, 2),
            PAIR,
            whole(TOK, model),
            pl.BlockSpec((2 * SIZE, model), lambda h: (h, 0)),
        ],
        out_specs=[PAIR, PAIR, PAIR, PAIR, cols(2 * WINDOW, 2)],
        out_shape=[wide32, wide16, wide16, wide16, edge16],
        compiler_params=params(12),
        name="window_grad",
    )(query, key, value, before, probs, grad_rows, out_weight)

    prefix, grad, win_key, win_value, edge_grad = after(
        prefix, grad, win_key, win_value, edge_grad
    )
    prefix = prefix.reshape(HEADS * ROWS, SIZE)

    mixed, grad_linear, grad_state = pl.pallas_call(
        mix_kernel,
        grid=(HEADS,),
        in_specs=[
            STATE, PHI, PHIT, COLS, COLS, COLS, COLS,
            pl.BlockSpec((1, SIZE), lambda h: (0, h)),
        ],
        out_specs=[COLS, COLS, STATE],
        out_shape=[wide16, wide16, states],
        compiler_params=params(8),
        name="mix",
    )(prefix, phi, phit, local, attended, grad, cum, norm_gain.reshape(1, width))

    arrived = swap(grad_state.reshape(chunks))

    returned = lax.ppermute(edge_grad, "seq", [(i + 1, i) for i in range(peers - 1)])
    partial = jnp.dot(mixed, out_weight, preferred_element_type=F32).astype(BF16)
    partial = partial.reshape(ways, count // ways, model)

    def piece_for(k):
        return lax.dynamic_index_in_dim(partial, (lane + k) % ways, 0, keepdims=False)

    sums = [piece_for(0)] + [shifted(piece_for(k), ways, k) for k in range(1, ways)]

    arrived, *sums = after(arrived, *sums)
    suffix = swap(chain(arrived, True))

    gq_t, gk_local, gv_local = pl.pallas_call(
        intra_grad_kernel,
        grid=(HEADS,),
        in_specs=[FEATS, FEATS, COLS, COLS, CROW, SEL, SEL_T, STATE, COLS],
        out_specs=[FEATS, FEATS, COLS],
        out_shape=[
            shape((HEADS * FEAT, TOK), BF16),
            shape((HEADS * FEAT, TOK), F32),
            wide32,
        ],
        compiler_params=params(8),
        name="intra_grad",
    )(fq_t, fk_t, value, cum, cum_row, sel_q, sel_qt, prefix, grad_linear)
    layer_out = sum(p.astype(F32) for p in sums).astype(BF16)

    suffix, gk_local, gv_local, layer_out = after(suffix, gk_local, gv_local, layer_out)

    grad_key, grad_value, gfk_t = pl.pallas_call(
        finish_kernel,
        grid=(HEADS,),
        in_specs=[
            FEATS, COLS, COLS, SEL, SEL_T, STATE, COLS, FEATS, COLS, COLS, cols(2 * WINDOW),
        ],
        out_specs=[COLS, COLS, FEATS],
        out_shape=[wide16, wide16, shape((HEADS * FEAT, TOK), BF16)],
        compiler_params=params(8),
        name="finish",
    )(
        fk_t, value, cum, sel_k, sel_kt, suffix.reshape(HEADS * ROWS, SIZE), gv_local, gk_local,
        win_key, win_value, returned,
    )
    return (layer_out, grad_query, grad_key, grad_value, gq_t.T, gfk_t.T)


def solution(mesh):
    return jax.shard_map(
        body,
        mesh=mesh,
        in_specs=(
            P("seq", "mp"),
            P("seq", "mp"),
            P("seq", "mp"),
            P("seq", "mp"),
            P("seq", "mp"),
            P("mp", "seq"),
            P("seq"),
            P("mp"),
            P("mp", None),
            P(("seq", "mp"), None),
        ),
        out_specs=(
            P(("seq", "mp"), None),
            P("seq", "mp"),
            P("seq", "mp"),
            P("seq", "mp"),
            P("seq", "mp"),
            P("seq", "mp"),
        ),
        check_vma=False,
    )
```

profile of v0, /device:TPU:1, one launch (start us, length us, event | category | flops | bytes accessed | tf_op | source)
XLA Modules:
  0.0 138.4 jit_solution(15818631056167005771)
XLA Ops:
  0.6 2.1 %collective-permute-start.1 = (bf16[64,2048]{1,0:T(8,128)(2,1)}, bf16[64,2048]{1,0:T(8,128)(2,1)}, u32[]{:S(2)}, u32[]{:S(2)}) collective-permute-start(bf16[64,2048]{1,0:T(8,128)(2,1)} %param.23), channel_id=1, source_target_pairs={{0,1},{1,2},{2,3},{3,0},{4,5},{5,6},{6,7},{7,4},{8,9},{9,10},{10,1... | collective-permute-start | bytes 786440 | tf_op jit(solution)/shard_map/ppermute | solution.py:306
  2.8 2.5 %collective-permute-start.2 = (bf16[64,2048]{1,0:T(8,128)(2,1)}, bf16[64,2048]{1,0:T(8,128)(2,1)}, u32[]{:S(2)}, u32[]{:S(2)}) collective-permute-start(bf16[64,2048]{1,0:T(8,128)(2,1)} %param.23), channel_id=1, source_target_pairs={{0,2},{1,3},{2,0},{3,1},{4,6},{5,7},{6,4},{7,5},{8,10},{9,11},{10,... | collective-permute-start | bytes 786440 | tf_op jit(solution)/shard_map/ppermute | solution.py:306
  5.2 1.2 collective-permute-start.3
  10.7 2.2 %local_state.1 = (bf16[1024,128]{1,0:T(8,128)(2,1)}, f32[256,512]{1,0:T(8,128)S(1)}, f32[4,1,256]{2,1,0:T(1,128)S(1)}, bf16[128,512]{1,0:T(8,128)(2,1)}) custom-call(bf16[64,256]{1,0:T(8,128)(2,1)S(1)} %bitcast.33, bf16[256,512]{1,0:T(8,128)(2,1)S(1)} %copy-done, bf16[256,512]{1,0:T(8,128)(2,1)S(1)} %copy-done.3, f32[4,256]{1,0:T(4,128)S(1)} %copy-done.37, ...), custom_call_target="tpu_custom_call" | custom-call | tf_op jit(solution)/shard_map/local_state/pallas_call | solution.py:326
  12.9 4.9 %collective-permute-start = (bf16[128,512]{1,0:T(8,128)(2,1)}, bf16[128,512]{1,0:T(8,128)(2,1)}, u32[]{:S(2)}, u32[]{:S(2)}) collective-permute-start(bf16[128,512]{1,0:T(8,128)(2,1)} %get-tuple-element.50), channel_id=1, source_target_pairs={{0,4},{4,8},{8,12},{12,16},{16,20},{20,24},{24,28},{28,32},{32,36}... | collective-permute-start | bytes 393224 | tf_op jit(solution)/shard_map/ppermute | solution.py:349
  17.8 11.1 %all-to-all-start = ((bf16[64,16,128]{2,1,0:T(8,128)(2,1)}), bf16[64,16,128]{2,1,0:T(8,128)(2,1)}, u32[]{:S(2)}, u32[]{:S(2)}) async-start(bf16[64,16,128]{2,1,0:T(8,128)(2,1)} %bitcast.1), calls=%async_computation | async-start | bytes 524288 | tf_op jit(solution)/shard_map/all_to_all | solution.py:288
  31.9 2.0 %intra.1 = (f32[256,512]{1,0:T(8,128)S(1)}, bf16[256,1024]{1,0:T(8,128)(2,1)S(1)}, bf16[1024,256]{1,0:T(8,128)(2,1)S(1)}) custom-call(bf16[64,256]{1,0:T(8,128)(2,1)S(1)} %bitcast.38, bf16[64,256]{1,0:T(8,128)(2,1)S(1)} %bitcast.34, bf16[256,512]{1,0:T(8,128)(2,1)S(1)} %copy-done.1, f32[256,512]{1,0:T(8,128)S(1)} %get-tuple-element.53.cum, ...), custom_call_target="tpu_custom_call" | custom-call | tf_op jit(solution)/shard_map/intra/pallas_call | solution.py:352
  35.5 6.4 %window.1 = (f32[256,512]{1,0:T(8,128)S(1)}, bf16[256,512]{1,0:T(8,128)(2,1)S(1)}) custom-call(s32[5]{0:T(128)S(1)} %pad_add_fusion.band, bf16[256,512]{1,0:T(8,128)(2,1)S(1)} %copy-done.5, bf16[256,512]{1,0:T(8,128)(2,1)S(1)} %copy-done.4, bf16[256,512]{1,0:T(8,128)(2,1)S(1)} %copy-done.1, bf16[128,512]{1,0:T(8,128)(2,1)} %collective-permute-done.before), custom_call_target="tpu_custom_call" | custom-call | tf_op jit(solution)/shard_map/window/pallas_call | solution.py:364
  43.4 1.7 %bitcast_dynamic-update-slice_fusion.2 = bf16[4,64,2048]{2,1,0:T(8,128)(2,1)} fusion(bf16[4,64,2048]{2,1,0:T(8,128)(2,1)} %bitcast_dynamic-update-slice_fusion.3, s32[]{:T(128)S(6)} %select_n.64, bf16[64,2048]{1,0:T(8,128)(2,1)} %collective-permute-done.1), kind=kLoop, calls=%fused_computation.4 | loop fusion | bytes 524292 | tf_op jit(solution)/shard_map/dynamic_update_slice | solution.py:387
  46.9 10.3 %all-to-all-start.1 = ((bf16[64,16,128]{2,1,0:T(8,128)(2,1)}), bf16[64,16,128]{2,1,0:T(8,128)(2,1)S(1)}, u32[]{:S(2)}, u32[]{:S(2)}) async-start(bf16[64,16,128]{2,1,0:T(8,128)(2,1)} %copy-done.7), calls=%async_computation.1 | async-start | bytes 524288 | tf_op jit(solution)/shard_map/all_to_all | solution.py:288
  57.2 1.7 %bitcast_dynamic-update-slice_fusion.1 = bf16[4,64,2048]{2,1,0:T(8,128)(2,1)} fusion(bf16[4,64,2048]{2,1,0:T(8,128)(2,1)} %bitcast_dynamic-update-slice_fusion.2, s32[]{:T(128)S(6)} %select_n.66, bf16[64,2048]{1,0:T(8,128)(2,1)} %collective-permute-done.2), kind=kLoop, calls=%fused_computation.3 | loop fusion | bytes 524292 | tf_op jit(solution)/shard_map/dynamic_update_slice | solution.py:387
  58.9 1.7 %bitcast_dynamic-update-slice_fusion = bf16[4,64,2048]{2,1,0:T(8,128)(2,1)} fusion(bf16[4,64,2048]{2,1,0:T(8,128)(2,1)} %bitcast_dynamic-update-slice_fusion.1, s32[]{:T(128)S(6)} %select_n.68, bf16[64,2048]{1,0:T(8,128)(2,1)} %collective-permute-done.3), kind=kLoop, calls=%fused_computation.2 | loop fusion | bytes 524292 | tf_op jit(solution)/shard_map/dynamic_update_slice | solution.py:387
  62.5 8.4 %window_grad.1 = (f32[256,512]{1,0:T(8,128)S(1)}, bf16[256,512]{1,0:T(8,128)(2,1)}, bf16[256,512]{1,0:T(8,128)(2,1)S(1)}, bf16[256,512]{1,0:T(8,128)(2,1)S(1)}, bf16[128,512]{1,0:T(8,128)(2,1)S(1)}) custom-call(bf16[256,512]{1,0:T(8,128)(2,1)S(1)} %copy-done.6, bf16[256,512]{1,0:T(8,128)(2,1)S(1)} %copy-done.4, bf16[256,512]{1,0:T(8,128)(2,1)S(1)} %copy-done.1, ...), custom_call_target="tpu_custom_call" | custom-call | tf_op jit(solution)/shard_map/window_grad/pallas_call | solution.py:390
  79.0 2.4 %mix.1 = (bf16[256,512]{1,0:T(8,128)(2,1)S(1)}, bf16[256,512]{1,0:T(8,128)(2,1)S(1)}, bf16[1024,128]{1,0:T(8,128)(2,1)S(1)}) custom-call(bf16[1024,128]{1,0:T(8,128)(2,1)S(1)} %bitcast.30, bf16[256,1024]{1,0:T(8,128)(2,1)S(1)} %copy-done.17, bf16[1024,256]{1,0:T(8,128)(2,1)S(1)} %copy-done.19, f32[256,512]{1,0:T(8,128)S(1)} %copy-done.15, ...), custom_call_target="tpu_custom_call" | custom-call | tf_op jit(solution)/shard_map/mix/pallas_call | solution.py:413
  82.9 10.3 %all-to-all-start.2 = ((bf16[64,16,128]{2,1,0:T(8,128)(2,1)}), bf16[64,16,128]{2,1,0:T(8,128)(2,1)S(1)}, u32[]{:S(2)}, u32[]{:S(2)}) async-start(bf16[64,16,128]{2,1,0:T(8,128)(2,1)} %bitcast.37), calls=%async_computation.2 | async-start | bytes 524288 | tf_op jit(solution)/shard_map/all_to_all | solution.py:288
  93.3 1.7 %convolution_convert_fusion = bf16[256,2048]{1,0:T(8,128)(2,1)S(1)} fusion(bf16[256,512]{1,0:T(8,128)(2,1)} %copy-done.33, bf16[512,2048]{1,0:T(8,128)(2,1)S(1)} %copy-done.2), kind=kOutput, calls=%fused_computation | convolution fusion | flops 537395200 | bytes 3407872 | tf_op jit(solution)/shard_map/dot_general | solution.py:429
  96.1 1.9 %collective-permute-start.6 = (bf16[64,2048]{1,0:T(8,128)(2,1)S(1)}, bf16[64,2048]{1,0:T(8,128)(2,1)}, u32[]{:S(2)}, u32[]{:S(2)}) collective-permute-start(bf16[64,2048]{1,0:T(8,128)(2,1)S(1)} %get-tuple-element.92), channel_id=1, source_target_pairs={{0,3},{1,0},{2,1},{3,2},{4,7},{5,4},{6,5},{7,6},{8,11},{9,8},{10,9... | collective-permute-start | bytes 786440 | tf_op jit(solution)/shard_map/ppermute | solution.py:306
  98.0 11.5 %collective-permute-done.4 = bf16[64,2048]{1,0:T(8,128)(2,1)} collective-permute-done((bf16[64,2048]{1,0:T(8,128)(2,1)S(1)}, bf16[64,2048]{1,0:T(8,128)(2,1)}, u32[]{:S(2)}, u32[]{:S(2)}) %collective-permute-start.4) | collective-permute-done | bytes 262176 | tf_op jit(solution)/shard_map/ppermute | solution.py:306
  111.1 11.3 %all-to-all-start.3 = ((bf16[64,16,128]{2,1,0:T(8,128)(2,1)}), bf16[64,16,128]{2,1,0:T(8,128)(2,1)S(1)}, u32[]{:S(2)}, u32[]{:S(2)}) async-start(bf16[64,16,128]{2,1,0:T(8,128)(2,1)} %chain_back.1), calls=%async_computation.3 | async-start | bytes 524288 | tf_op jit(solution)/shard_map/all_to_all | solution.py:288
  122.4 4.1 %intra_grad.1 = (bf16[64,256]{1,0:T(8,128)(2,1)}, f32[64,256]{1,0:T(8,128)S(1)}, f32[256,512]{1,0:T(8,128)S(1)}) custom-call(bf16[64,256]{1,0:T(8,128)(2,1)S(1)} %bitcast.39, bf16[64,256]{1,0:T(8,128)(2,1)S(1)} %bitcast.35, bf16[256,512]{1,0:T(8,128)(2,1)S(1)} %copy-done.1, f32[256,512]{1,0:T(8,128)S(1)} %get-tuple-element.53.cum, ...), custom_call_target="tpu_custom_call" | custom-call | tf_op jit(solution)/shard_map/intra_grad/pallas_call | solution.py:440
  126.5 2.4 %collective-permute-start.7 = (bf16[128,512]{1,0:T(8,128)(2,1)S(1)}, bf16[128,512]{1,0:T(8,128)(2,1)S(1)}, u32[]{:S(2)}, u32[]{:S(2)}) collective-permute-start(bf16[128,512]{1,0:T(8,128)(2,1)S(1)} %copy-done.40), channel_id=1, source_target_pairs={{4,0},{8,4},{12,8},{16,12},{20,16},{24,20},{28,24},{32,28},{36,32}... | collective-permute-start | bytes 393224 | tf_op jit(solution)/shard_map/ppermute | solution.py:428
  128.9 1.9 %add_convert_fusion = bf16[64,2048]{1,0:T(8,128)(2,1)} fusion(bf16[64,2048]{1,0:T(8,128)(2,1)} %collective-permute-done.6, bf16[64,2048]{1,0:T(8,128)(2,1)} %copy-done.41, bf16[64,2048]{1,0:T(8,128)(2,1)} %collective-permute-done.4, bf16[64,2048]{1,0:T(8,128)(2,1)S(1)} %get-tuple-element.76), kind=kLoop, calls=%fused_computation.1 | loop fusion | flops 1048576 | bytes 1310720 | tf_op jit(solution)/shard_map/convert_element_type | solution.py:453
  130.8 3.6 %all-to-all-done.3 = bf16[64,16,128]{2,1,0:T(8,128)(2,1)S(1)} async-done(((bf16[64,16,128]{2,1,0:T(8,128)(2,1)}), bf16[64,16,128]{2,1,0:T(8,128)(2,1)S(1)}, u32[]{:S(2)}, u32[]{:S(2)}) %all-to-all-start.3) | async-done | bytes 262176 | tf_op jit(solution)/shard_map/all_to_all | solution.py:288
  134.4 4.0 %finish.1 = (bf16[256,512]{1,0:T(8,128)(2,1)}, bf16[256,512]{1,0:T(8,128)(2,1)}, bf16[64,256]{1,0:T(8,128)(2,1)}) custom-call(bf16[64,256]{1,0:T(8,128)(2,1)S(1)} %bitcast.36, bf16[256,512]{1,0:T(8,128)(2,1)S(1)} %copy-done.1, f32[256,512]{1,0:T(8,128)S(1)} %get-tuple-element.53.cum, bf16[512,16]{1,0:T(8,128)(2,1)S(1)} %copy-done.13, ...), custom_call_target="tpu_custom_call" | custom-call | tf_op jit(solution)/shard_map/finish/pallas_call | solution.py:457
  (106 shorter events, 26.1 us)
Async XLA Ops:
  0.6 30.2 %copy-start.43 = (s32[4]{0:T(128)S(1)}, s32[4]{0:T(128)}, u32[]{:S(2)}) copy-start(s32[4]{0:T(128)} %param.20) | copy-start | bytes 52
  0.6 42.8 %collective-permute-start.1 = (bf16[64,2048]{1,0:T(8,128)(2,1)}, bf16[64,2048]{1,0:T(8,128)(2,1)}, u32[]{:S(2)}, u32[]{:S(2)}) collective-permute-start(bf16[64,2048]{1,0:T(8,128)(2,1)} %param.23), channel_id=1, source_target_pairs={{0,1},{1,2},{2,3},{3,0},{4,5},{5,6},{6,7},{7,4},{8,9},{9,10},{10,1... | collective-permute-start | bytes 786440 | tf_op jit(solution)/shard_map/ppermute | solution.py:306
  2.8 54.4 %collective-permute-start.2 = (bf16[64,2048]{1,0:T(8,128)(2,1)}, bf16[64,2048]{1,0:T(8,128)(2,1)}, u32[]{:S(2)}, u32[]{:S(2)}) collective-permute-start(bf16[64,2048]{1,0:T(8,128)(2,1)} %param.23), channel_id=1, source_target_pairs={{0,2},{1,3},{2,0},{3,1},{4,6},{5,7},{6,4},{7,5},{8,10},{9,11},{10,... | collective-permute-start | bytes 786440 | tf_op jit(solution)/shard_map/ppermute | solution.py:306
  5.2 53.7 %collective-permute-start.3 = (bf16[64,2048]{1,0:T(8,128)(2,1)}, bf16[64,2048]{1,0:T(8,128)(2,1)}, u32[]{:S(2)}, u32[]{:S(2)}) collective-permute-start(bf16[64,2048]{1,0:T(8,128)(2,1)} %param.23), channel_id=1, source_target_pairs={{0,3},{1,0},{2,1},{3,2},{4,7},{5,4},{6,5},{7,6},{8,11},{9,8},{10,9... | collective-permute-start | bytes 786440 | tf_op jit(solution)/shard_map/ppermute | solution.py:306
  10.6 20.3 %copy-start.35 = (bf16[16,512]{1,0:T(8,128)(2,1)S(1)}, bf16[16,512]{1,0:T(8,128)(2,1)}, u32[]{:S(2)}) copy-start(bf16[16,512]{1,0:T(8,128)(2,1)} %constant.85.clone.sel_t) | copy-start | bytes 49156
  10.6 24.9 %copy-start.4 = (bf16[256,512]{1,0:T(8,128)(2,1)S(1)}, bf16[256,512]{1,0:T(8,128)(2,1)}, u32[]{:S(2)}) copy-start(bf16[256,512]{1,0:T(8,128)(2,1)} %key.3) | copy-start | bytes 786436
  10.7 24.9 %copy-start.5 = (bf16[256,512]{1,0:T(8,128)(2,1)S(1)}, bf16[256,512]{1,0:T(8,128)(2,1)}, u32[]{:S(2)}) copy-start(bf16[256,512]{1,0:T(8,128)(2,1)} %query.3) | copy-start | bytes 786436
  12.9 22.6 %collective-permute-start = (bf16[128,512]{1,0:T(8,128)(2,1)}, bf16[128,512]{1,0:T(8,128)(2,1)}, u32[]{:S(2)}, u32[]{:S(2)}) collective-permute-start(bf16[128,512]{1,0:T(8,128)(2,1)} %get-tuple-element.50), channel_id=1, source_target_pairs={{0,4},{4,8},{8,12},{12,16},{16,20},{20,24},{24,28},{28,32},{32,36}... | collective-permute-start | bytes 393224 | tf_op jit(solution)/shard_map/ppermute | solution.py:349
  17.8 27.2 %all-to-all-start = ((bf16[64,16,128]{2,1,0:T(8,128)(2,1)}), bf16[64,16,128]{2,1,0:T(8,128)(2,1)}, u32[]{:S(2)}, u32[]{:S(2)}) async-start(bf16[64,16,128]{2,1,0:T(8,128)(2,1)} %bitcast.1), calls=%async_computation | async-start | bytes 524288 | tf_op jit(solution)/shard_map/all_to_all | solution.py:288
  31.9 28.7 %copy-start.2 = (bf16[512,2048]{1,0:T(8,128)(2,1)S(1)}, bf16[512,2048]{1,0:T(8,128)(2,1)}, u32[]{:S(2)}) copy-start(bf16[512,2048]{1,0:T(8,128)(2,1)} %weight.1) | copy-start | bytes 6291460
  46.9 26.9 %all-to-all-start.1 = ((bf16[64,16,128]{2,1,0:T(8,128)(2,1)}), bf16[64,16,128]{2,1,0:T(8,128)(2,1)S(1)}, u32[]{:S(2)}, u32[]{:S(2)}) async-start(bf16[64,16,128]{2,1,0:T(8,128)(2,1)} %copy-done.7), calls=%async_computation.1 | async-start | bytes 524288 | tf_op jit(solution)/shard_map/all_to_all | solution.py:288
  82.9 27.3 %all-to-all-start.2 = ((bf16[64,16,128]{2,1,0:T(8,128)(2,1)}), bf16[64,16,128]{2,1,0:T(8,128)(2,1)S(1)}, u32[]{:S(2)}, u32[]{:S(2)}) async-start(bf16[64,16,128]{2,1,0:T(8,128)(2,1)} %bitcast.37), calls=%async_computation.2 | async-start | bytes 524288 | tf_op jit(solution)/shard_map/all_to_all | solution.py:288
  95.0 27.4 %copy-start.11 = (bf16[512,16]{1,0:T(8,128)(2,1)S(1)}, bf16[512,16]{1,0:T(8,128)(2,1)}, u32[]{:S(2)}) copy-start(bf16[512,16]{1,0:T(8,128)(2,1)} %constant.84.clone.sel) | copy-start | bytes 49156
  95.0 27.4 %copy-start.32 = (bf16[256,512]{1,0:T(8,128)(2,1)S(1)}, bf16[256,512]{1,0:T(8,128)(2,1)}, u32[]{:S(2)}) copy-start(bf16[256,512]{1,0:T(8,128)(2,1)} %copy-done.31) | copy-start | bytes 786436
  95.0 31.5 %copy-start.40 = (bf16[128,512]{1,0:T(8,128)(2,1)S(1)}, bf16[128,512]{1,0:T(8,128)(2,1)}, u32[]{:S(2)}) copy-start(bf16[128,512]{1,0:T(8,128)(2,1)} %copy-done.39) | copy-start | bytes 393220
  95.1 39.3 %copy-start.13 = (bf16[512,16]{1,0:T(8,128)(2,1)S(1)}, bf16[512,16]{1,0:T(8,128)(2,1)}, u32[]{:S(2)}) copy-start(bf16[512,16]{1,0:T(8,128)(2,1)} %constant.82.clone.sel) | copy-start | bytes 49156
  95.1 39.3 %copy-start.25 = (bf16[256,512]{1,0:T(8,128)(2,1)S(1)}, bf16[256,512]{1,0:T(8,128)(2,1)}, u32[]{:S(2)}) copy-start(bf16[256,512]{1,0:T(8,128)(2,1)} %copy-done.24) | copy-start | bytes 786436
  95.1 39.3 %copy-start.27 = (bf16[256,512]{1,0:T(8,128)(2,1)S(1)}, bf16[256,512]{1,0:T(8,128)(2,1)}, u32[]{:S(2)}) copy-start(bf16[256,512]{1,0:T(8,128)(2,1)} %copy-done.26) | copy-start | bytes 786436
  95.1 39.3 %copy-start.36 = (bf16[16,512]{1,0:T(8,128)(2,1)S(1)}, bf16[16,512]{1,0:T(8,128)(2,1)}, u32[]{:S(2)}) copy-start(bf16[16,512]{1,0:T(8,128)(2,1)} %constant.83.clone.sel_t) | copy-start | bytes 49156
  95.1 14.4 %collective-permute-start.4 = (bf16[64,2048]{1,0:T(8,128)(2,1)S(1)}, bf16[64,2048]{1,0:T(8,128)(2,1)}, u32[]{:S(2)}, u32[]{:S(2)}) collective-permute-start(bf16[64,2048]{1,0:T(8,128)(2,1)S(1)} %get-tuple-element.94), channel_id=1, source_target_pairs={{0,1},{1,2},{2,3},{3,0},{4,5},{5,6},{6,7},{7,4},{8,9},{9,10},{10,1... | collective-permute-start | bytes 786440 | tf_op jit(solution)/shard_map/ppermute | solution.py:306
  95.5 14.0 %collective-permute-start.5 = (bf16[64,2048]{1,0:T(8,128)(2,1)S(1)}, bf16[64,2048]{1,0:T(8,128)(2,1)S(1)}, u32[]{:S(2)}, u32[]{:S(2)}) collective-permute-start(bf16[64,2048]{1,0:T(8,128)(2,1)S(1)} %get-tuple-element.93), channel_id=1, source_target_pairs={{0,2},{1,3},{2,0},{3,1},{4,6},{5,7},{6,4},{7,5},{8,10},{9,11},{10,... | collective-permute-start | bytes 786440 | tf_op jit(solution)/shard_map/ppermute | solution.py:306
  96.1 14.2 %collective-permute-start.6 = (bf16[64,2048]{1,0:T(8,128)(2,1)S(1)}, bf16[64,2048]{1,0:T(8,128)(2,1)}, u32[]{:S(2)}, u32[]{:S(2)}) collective-permute-start(bf16[64,2048]{1,0:T(8,128)(2,1)S(1)} %get-tuple-element.92), channel_id=1, source_target_pairs={{0,3},{1,0},{2,1},{3,2},{4,7},{5,4},{6,5},{7,6},{8,11},{9,8},{10,9... | collective-permute-start | bytes 786440 | tf_op jit(solution)/shard_map/ppermute | solution.py:306
  111.1 23.3 %all-to-all-start.3 = ((bf16[64,16,128]{2,1,0:T(8,128)(2,1)}), bf16[64,16,128]{2,1,0:T(8,128)(2,1)S(1)}, u32[]{:S(2)}, u32[]{:S(2)}) async-start(bf16[64,16,128]{2,1,0:T(8,128)(2,1)} %chain_back.1), calls=%async_computation.3 | async-start | bytes 524288 | tf_op jit(solution)/shard_map/all_to_all | solution.py:288
  126.5 7.9 %collective-permute-start.7 = (bf16[128,512]{1,0:T(8,128)(2,1)S(1)}, bf16[128,512]{1,0:T(8,128)(2,1)S(1)}, u32[]{:S(2)}, u32[]{:S(2)}) collective-permute-start(bf16[128,512]{1,0:T(8,128)(2,1)S(1)} %copy-done.40), channel_id=1, source_target_pairs={{4,0},{8,4},{12,8},{16,12},{20,16},{24,20},{28,24},{32,28},{36,32}... | collective-permute-start | bytes 393224 | tf_op jit(solution)/shard_map/ppermute | solution.py:428
  (32 other events, 119.9 us)
where the time goes:
time: 140 us; the launch traced here: 138 us
  starting transfers between devices  58.9 us (42%)
  Pallas kernels  31.5 us (22%)
  local copies, waits for them, and re-layouts  28.1 us (20%)
  waiting for transfers between devices  15.2 us (11%)
  other arithmetic  2.02 us (1%)
  matrix products  1.66 us (1%)
    all_to_all x4, starting transfers between devices, swap(): return lax.all_to_all(value, 'seq', split_axis=0, concat_axis=0, tiled=True)  43 us
    unnamed x88, local copies, waits for them, and re-layouts  21.1 us
    ppermute x6, waiting for transfers between devices, shifted(): return lax.ppermute(value, 'mp', [(i, (i + k) % ways) for i in range(ways)])  11.6 us
    ppermute x6, starting transfers between devices, shifted(): return lax.ppermute(value, 'mp', [(i, (i + k) % ways) for i in range(ways)])  8.61 us
    pallas_call x1, Pallas kernels, body(): pl.pallas_call(window_grad_kernel, grid=(HEADS // 2,), in_specs=[PAIR, PA...  8.44 us
    pallas_call x1, Pallas kernels, body(): pl.pallas_call(window_kernel, grid=(HEADS // 2,), in_specs=[pl.BlockSpec(...  6.37 us
    dynamic_update_slice x4, local copies, waits for them, and re-layouts, body(): lax.dynamic_update_slice(grad_rows, piece[None], ((lane - k) % ways, 0, 0))  5.76 us
    ppermute x1, starting transfers between devices, body(): before = lax.ppermute(edge, 'seq', [(i, i + 1) for i in range(peers - 1)])  4.94 us
  transfers between devices with their start and end apart: 12, of which 2 were waited for; matrix products, arithmetic and copies ran while one was open for 8% of the time, Pallas kernels for 18%

commit v1 on v0

v1 whole, which is shorter than its diff:
```python
import numpy as np
import ml_dtypes
import jax
import jax.numpy as jnp
from jax import lax
from jax.experimental import pallas as pl
from jax.experimental.pallas import tpu as pltpu
from jax.sharding import PartitionSpec as P

WINDOW = 64
EPS = 1e-06
NEG = -1e30
F32 = jnp.float32
BF16 = jnp.bfloat16
TOK = 256
HEADS = 4
SIZE = 128
FEAT = 16
ROWS = 256
SCALE = SIZE**-0.5

NN = (((1,), (0,)), ((), ()))
NT = (((1,), (1,)), ((), ()))
TN = (((0,), (0,)), ((), ()))


def mm(a, b, dims):
    return lax.dot_general(a, b, dims, preferred_element_type=F32)


def selectors(query_side):
    first = np.zeros((ROWS, FEAT), np.float32)
    second = np.zeros_like(first)
    weight = [1 / 32] + [1 / 16] * 7 + [1 / 32, 1 / 4]
    for a in range(FEAT):
        for r in range(10):
            first[a * 16 + r, a] = weight[r] if query_side else 1.0
            if r < 9:
                second[a * 16 + r, (a + r) % FEAT] = 1.0
    both = np.concatenate([first, second], axis=0).astype(ml_dtypes.bfloat16)
    return (both, np.ascontiguousarray(both.T))


SEL_K, SEL_K_T = selectors(False)
SEL_Q, SEL_Q_T = selectors(True)


def row_kind(shape, dim):
    return lax.broadcasted_iota(jnp.int32, shape, dim) % 16


def factors_rows(feats_t, sel, const):
    both = mm(sel, feats_t, NN)
    kind = row_kind((ROWS, 1), 0)
    left = both[:ROWS, :] + jnp.where(kind == 10, const, 0.0)
    right = both[ROWS:, :] + jnp.where((kind == 9) | (kind == 10), 1.0, 0.0)
    return (left, right)


def factors_cols(feats_t, sel_t, const):
    both = mm(feats_t, sel_t, TN)
    kind = row_kind((1, ROWS), 1)
    left = both[:, :ROWS] + jnp.where(kind == 10, const, 0.0)
    right = both[:, ROWS:] + jnp.where((kind == 9) | (kind == 10), 1.0, 0.0)
    return (left, right)


def feature_grad(grad_phi, left, right, sel_t):
    both = jnp.concatenate([grad_phi * right, grad_phi * left], axis=0)
    return mm(sel_t, both.astype(BF16), NN)


def split3(value):
    hi = value.astype(BF16)
    rest = value - hi.astype(F32)
    mid = rest.astype(BF16)
    low = (rest - mid.astype(F32)).astype(BF16)
    return (hi, mid, low)


def with_total(state, total):
    kind = row_kind((ROWS, 1), 0)
    hi, mid, low = split3(total)
    state = jnp.where(kind == 11, hi.astype(F32), state)
    state = jnp.where(kind == 12, mid.astype(F32), state)
    return jnp.where(kind == 13, low.astype(F32), state)


def head_cols(h):
    return slice(h * SIZE, (h + 1) * SIZE)


def head_rows(h):
    return slice(h * ROWS, (h + 1) * ROWS)


def head_feats(h):
    return slice(h * FEAT, (h + 1) * FEAT)


def local_state_kernel(
    feat_t, decay, sel, value_far, key_far, query_far,
    state_out, cum_out, cum_row_out, edge_out, faded_out, value, key, query, sems
):
    first = pltpu.make_async_copy(value_far, value, sems.at[0])
    first.start()
    others = [
        pltpu.make_async_copy(far, near, sems.at[1 + i])
        for i, (far, near) in enumerate(((key_far, key), (query_far, query)))
    ]
    for copy in others:
        copy.start()
    tri = (
        lax.broadcasted_iota(jnp.int32, (TOK, TOK), 0)
        >= lax.broadcasted_iota(jnp.int32, (TOK, TOK), 1)
    ).astype(F32).astype(BF16)
    parts = split3(decay[...])
    cum_row_out[:, 0, :] = sum(mm(p, tri, NT) for p in parts)
    cum_all = sum(mm(tri, p, NT) for p in parts)
    cum_out[...] = cum_all
    first.wait()
    for h in range(HEADS):
        cum = cum_all[:, h : h + 1]
        total = cum[TOK - 1 : TOK, :]
        left, right = factors_rows(feat_t[head_feats(h), :], sel[...], 1.0)
        phi = (left * right).astype(BF16)
        faded = (value[:, head_cols(h)].astype(F32) * jnp.exp(total - cum)).astype(BF16)
        faded_out[:, head_cols(h)] = faded
        state = mm(phi, faded, NN)
        state_out[head_rows(h), :] = with_total(state, total).astype(BF16)
    for copy in others:
        copy.wait()
    edge_out[:WINDOW, :] = key[TOK - WINDOW :, :]
    edge_out[WINDOW:, :] = value[TOK - WINDOW :, :]


def chain_kernel(reverse, arrived, before_out):
    count = arrived.shape[0]
    carry = jnp.zeros((16, SIZE), F32)
    order = range(count)
    for j in reversed(order) if reverse else order:
        before_out[j] = carry.astype(BF16)
        piece = arrived[j].astype(F32)
        total = piece[11:12] + piece[12:13] + piece[13:14]
        carry = carry * jnp.exp(total) + piece


def intra_weights(fq_t, fk_t, cum, cum_row):
    inner = mm(fq_t, fk_t, TN) * FEAT**-0.5
    span = cum - cum_row
    causal = lax.broadcasted_iota(jnp.int32, (TOK, TOK), 0) >= lax.broadcasted_iota(
        jnp.int32, (TOK, TOK), 1
    )
    fade = jnp.where(causal, jnp.exp(jnp.minimum(span, 0.0)), 0.0)
    return (inner, fade, (1.0 + inner + 0.5 * inner * inner) * fade)


def block_pair(before, array, b):
    if b == 0:
        return jnp.concatenate([before, array[:WINDOW, :]], axis=0)
    return array[(b - 1) * WINDOW : (b + 1) * WINDOW, :]


def intra_kernel(fq_t, fk_t, value, cum, cum_row, sel, sel_t, local_out, phi_out, phit_out):
    for h in range(HEADS):
        feats = fq_t[head_feats(h), :]
        _, _, weights = intra_weights(
            feats, fk_t[head_feats(h), :], cum[:, h : h + 1], cum_row[h]
        )
        local_out[:, head_cols(h)] = mm(weights.astype(BF16), value[:, head_cols(h)], NN)
        left, right = factors_cols(feats, sel_t[...], 1 / 16)
        phi_out[:, head_rows(h)] = (left * right).astype(BF16)
        left, right = factors_rows(feats, sel[...], 1 / 16)
        phit_out[head_rows(h), :] = (left * right).astype(BF16)


def window_kernel(band, first_col, query, key, value, before, attended_out, probs_out):
    row = lax.broadcasted_iota(jnp.int32, (WINDOW, 2 * WINDOW), 0)
    col = lax.broadcasted_iota(jnp.int32, (WINDOW, 2 * WINDOW), 1)
    back = WINDOW + row - col
    for b in range(TOK // WINDOW):
        here = slice(b * WINDOW, (b + 1) * WINDOW)
        allowed = (back >= 0) & (back < band[b])
        if b == 0:
            allowed = allowed & (col >= first_col[0])
        for h in range(HEADS):
            cols = head_cols(h)
            keys = block_pair(before[:WINDOW, cols], key.at[:, cols], b)
            values = block_pair(before[WINDOW:, cols], value.at[:, cols], b)
            scores = mm(query[here, cols], keys, NT) * SCALE
            scores = jnp.where(allowed, scores, NEG)
            expo = jnp.exp(scores - jnp.max(scores, axis=-1, keepdims=True))
            probs = expo / jnp.sum(expo, axis=-1, keepdims=True)
            probs16 = probs.astype(BF16)
            probs_out[here, cols] = probs16
            attended_out[here, cols] = mm(probs16, values, NN).astype(BF16)


def window_grad_kernel(
    place, query, key, value, before, probs, piece0, piece1, piece2, piece3, weight_far,
    grad_out, gq_out, gk_out, gv_out, edge_out, rows, weight, sems
):
    pieces = (piece0, piece1, piece2, piece3)
    half = weight.shape[0] // 2
    copies = []
    for k, piece in enumerate(pieces):
        at = ((place[0] + (len(pieces) - k)) % len(pieces)) * WINDOW
        to = rows.at[pl.ds(pl.multiple_of(at, WINDOW), WINDOW), :]
        copies.append(pltpu.make_async_copy(piece, to, sems.at[k]))
    for i in range(2):
        part = slice(i * half, (i + 1) * half)
        copies.append(
            pltpu.make_async_copy(weight_far.at[part, :], weight.at[part, :], sems.at[4 + i])
        )
    for copy in copies:
        copy.start()
    for copy in copies[:5]:
        copy.wait()
    for h in range(HEADS):
        cols = head_cols(h)
        if h % 2 == 0:
            if h > 0:
                copies[5].wait()
            pair = slice(h * SIZE, (h + 2) * SIZE)
            grad16 = mm(rows[...], weight[pair, :], NT).astype(BF16)
            grad_out[:, pair] = grad16
        mine = head_cols(h % 2)
        key_parts = []
        value_parts = []
        for b in range(TOK // WINDOW):
            here = slice(b * WINDOW, (b + 1) * WINDOW)
            keys = block_pair(before[:WINDOW, cols], key.at[:, cols], b)
            values = block_pair(before[WINDOW:, cols], value.at[:, cols], b)
            probs16 = probs[here, cols]
            probs32 = probs16.astype(F32)
            grad_here = grad16[here, mine]
            grad_probs = mm(grad_here, values, NT).astype(BF16).astype(F32)
            along = jnp.sum(probs32 * grad_probs, axis=-1, keepdims=True)
            grad_scores = (probs32 * (grad_probs - along) * SCALE).astype(BF16)
            gq_out[here, cols] = mm(grad_scores, keys, NN).astype(BF16)
            key_parts.append(mm(grad_scores, query[here, cols], TN).astype(BF16))
            value_parts.append(mm(probs16, grad_here, TN).astype(BF16))
        for at, parts, out in ((0, key_parts, gk_out), (WINDOW, value_parts, gv_out)):
            edge_out[at : at + WINDOW, cols] = parts[0][:WINDOW, :]
            for b in range(TOK // WINDOW):
                own = parts[b][WINDOW:, :]
                if b + 1 < TOK // WINDOW:
                    own = own + parts[b + 1][:WINDOW, :]
                out[b * WINDOW : (b + 1) * WINDOW, cols] = own


def mix_kernel(
    state, phi, phit, local, attended, grad, cum, gain, grad_state_out, mixed_out, grad_linear_out
):
    for h in range(HEADS):
        cols = head_cols(h)
        steps = cum[:, h : h + 1]
        fade = jnp.exp(steps)
        linear = local[:, cols] + fade * mm(phi[:, head_rows(h)], state[head_rows(h), :], NN)
        scale = lax.rsqrt(jnp.mean(linear * linear, axis=-1, keepdims=True) + EPS)
        gains = gain[:, cols]
        mixed_out[:, cols] = (attended[:, cols].astype(F32) + linear * scale * gains).astype(BF16)
        scaled = grad[:, cols].astype(F32) * gains
        along = jnp.mean(scaled * linear, axis=-1, keepdims=True)
        grad_linear = scale * scaled - linear * (scale * scale * scale * along)
        grad_linear_out[:, cols] = grad_linear.astype(BF16)
        grad_state = mm(phit[head_rows(h), :], (grad_linear * fade).astype(BF16), NN)
        total = steps[TOK - 1 : TOK, :]
        grad_state_out[head_rows(h), :] = with_total(grad_state, total).astype(BF16)


def project_kernel(place, mixed, weight_far, piece0, piece1, piece2, piece3, rows, weight, sems):
    pieces = (piece0, piece1, piece2, piece3)
    step = weight.shape[1] // len(pieces)
    parts = [slice(i * step, (i + 1) * step) for i in range(len(pieces))]
    copies = [
        pltpu.make_async_copy(weight_far.at[:, part], weight.at[:, part], sems.at[i])
        for i, part in enumerate(parts)
    ]
    for copy in copies:
        copy.start()
    for k in range(len(pieces)):
        at = ((place[0] + k) % len(pieces)) * WINDOW
        rows[k * WINDOW : (k + 1) * WINDOW, :] = mixed[pl.ds(pl.multiple_of(at, WINDOW), WINDOW), :]
    for copy, part in zip(copies, parts):
        copy.wait()
        product = mm(rows[...], weight[:, part], NN).astype(BF16)
        for k, piece in enumerate(pieces):
            piece[:, part] = product[k * WINDOW : (k + 1) * WINDOW, :]


def intra_grad_kernel(
    fq_t, fk_t, value, cum, cum_row, sel, sel_t, state, grad_linear, gq_out, gk_out, gv_out
):
    for h in range(HEADS):
        cols = head_cols(h)
        fq, fk, grads = (fq_t[head_feats(h), :], fk_t[head_feats(h), :], grad_linear[:, cols])
        steps = cum[:, h : h + 1]
        inner, fade, weights = intra_weights(fq, fk, steps, cum_row[h])
        gv_out[:, cols] = mm(weights.astype(BF16), grads, TN)
        grad_inner = mm(grads, value[:, cols], NT) * fade * (1.0 + inner) * FEAT**-0.5
        grad_inner = grad_inner.astype(BF16)
        gk_out[head_feats(h), :] = mm(fq, grad_inner, NN)
        faded = (grads.astype(F32) * jnp.exp(steps)).astype(BF16)
        grad_phi = mm(state[head_rows(h), :], faded, NT)
        left, right = factors_rows(fq, sel[...], 1 / 16)
        gq = mm(fk, grad_inner, NT) + feature_grad(grad_phi, left, right, sel_t[...])
        gq_out[head_feats(h), :] = gq.astype(BF16)


def finish_kernel(
    fk_t, faded, cum, sel, sel_t, suffix, gv_local, gk_local, window_key, window_value, edge,
    gk_out, gv_out, gfk_out
):
    last = TOK - WINDOW
    gk_out[:last, :] = window_key[:last, :]
    gk_out[last:, :] = window_key[last:, :] + edge[:WINDOW, :]
    for h in range(HEADS):
        cols = head_cols(h)
        fk = fk_t[head_feats(h), :]
        steps = cum[:, h : h + 1]
        fade = jnp.exp(steps[TOK - 1 : TOK, :] - steps)
        left, right = factors_cols(fk, sel_t[...], 1.0)
        carried = mm((left * right).astype(BF16), suffix[head_rows(h), :], NN) * fade
        gv = (gv_local[:, cols] + carried).astype(BF16)
        gv_out[:last, cols] = window_value[:last, cols] + gv[:last, :]
        gv_out[last:, cols] = (window_value[last:, cols] + edge[WINDOW:, cols]) + gv[last:, :]
        grad_phi = mm(suffix[head_rows(h), :], faded[:, cols], NT)
        left, right = factors_rows(fk, sel[...], 1.0)
        gfk = gk_local[head_feats(h), :] + feature_grad(grad_phi, left, right, sel_t[...])
        gfk_out[head_feats(h), :] = gfk.astype(BF16)


HBM = pltpu.HBM
VMEM = pltpu.VMEM
NEAR = pl.BlockSpec(memory_space=pltpu.VMEM)
FAR = pl.BlockSpec(memory_space=pltpu.HBM)
ANYWHERE = pl.BlockSpec(memory_space=pl.ANY)
SCALARS = pl.BlockSpec(memory_space=pltpu.SMEM)


def params(mib):
    return pltpu.CompilerParams(vmem_limit_bytes=mib << 20)


def near(*values):
    return [pltpu.with_memory_space_constraint(v, pltpu.VMEM) for v in values]


def far(*values):
    return [pltpu.with_memory_space_constraint(v, pltpu.HBM) for v in values]


def kernel(body, name, ins, outs, mib=8, scratch=()):
    return pl.pallas_call(
        body,
        in_specs=ins,
        out_specs=[NEAR] * len(outs),
        out_shape=outs,
        scratch_shapes=list(scratch),
        compiler_params=params(mib),
        name=name,
    )


def swap(value):
    return lax.all_to_all(value, "seq", split_axis=0, concat_axis=0, tiled=True)


def chain(arrived, reverse):
    return kernel(
        lambda a, o: chain_kernel(reverse, a, o),
        "chain_back" if reverse else "chain_fwd",
        [NEAR],
        [HBM(arrived.shape, BF16)],
        4,
    )(*near(arrived))[0]


def after(value, *others):
    return lax.optimization_barrier((value, *others))


def shifted(value, ways, k):
    return lax.ppermute(value, "mp", [(i, (i + k) % ways) for i in range(ways)])


def body(
    query, key, value, feat_query, feat_key, log_decay, band_width, norm_gain, out_weight, grad_out
):
    count, width = query.shape
    peers = lax.axis_size("seq")
    place = lax.axis_index("seq")
    ways = lax.axis_size("mp")
    lane = lax.axis_index("mp").astype(jnp.int32)[None]
    consts = (jnp.asarray(m) for m in (SEL_K, SEL_K_T, SEL_Q, SEL_Q_T))
    sel_k, sel_kt, sel_q, sel_qt = far(*consts)
    fq_t, fk_t = far(feat_query.T, feat_key.T)
    chunks = (peers, HEADS * ROWS // peers, SIZE)
    states = (HEADS * ROWS, SIZE)
    model = grad_out.shape[1]

    value_arg = value
    state, cum, cum_row, edge, faded, value, key, query = kernel(
        local_state_kernel,
        "local_state",
        [NEAR] * 3 + [FAR] * 3,
        [
            HBM(states, BF16),
            VMEM((count, HEADS), F32),
            VMEM((HEADS, 1, TOK), F32),
            HBM((2 * WINDOW, width), BF16),
            HBM((count, width), BF16),
            VMEM(value.shape, BF16),
            VMEM(key.shape, BF16),
            VMEM(query.shape, BF16),
        ],
        8,
        [pltpu.SemaphoreType.DMA((3,))],
    )(fk_t, *far(log_decay), sel_k, *far(value, key, query))

    arrived = swap(state.reshape(chunks))

    before = lax.ppermute(edge, "seq", [(i, i + 1) for i in range(peers - 1)])
    pieces = [grad_out] + [shifted(grad_out, ways, k) for k in range(1, ways)]

    first_col = jnp.where(place == 0, WINDOW, 0).astype(jnp.int32)[None]
    attended, probs = kernel(
        window_kernel,
        "window",
        [SCALARS] * 2 + [NEAR] * 4,
        [VMEM((count, width), BF16), VMEM((count, width), BF16)],
    )(band_width, first_col, *near(query, key, value, before))

    arrived, attended, probs, *pieces = after(arrived, attended, probs, *pieces)
    chained, fq_late = after(chain(arrived, False), feat_query.T)
    prefix = swap(chained)

    local, phi, phit = kernel(
        intra_kernel,
        "intra",
        [NEAR] * 7,
        [
            VMEM((count, width), F32),
            VMEM((TOK, HEADS * ROWS), BF16),
            VMEM((HEADS * ROWS, TOK), BF16),
        ],
    )(*far(fq_late), fk_t, *near(value, cum, cum_row), sel_q, sel_qt)

    grad, grad_query, win_key, win_value, edge_grad = kernel(
        window_grad_kernel,
        "window_grad",
        [SCALARS] + [NEAR] * 5 + [ANYWHERE] * 4 + [FAR],
        [
            VMEM((count, width), BF16),
            HBM((count, width), BF16),
            HBM((count, width), BF16),
            HBM((count, width), BF16),
            HBM((2 * WINDOW, width), BF16),
        ],
        12,
        [
            pltpu.VMEM((count, model), BF16),
            pltpu.VMEM(out_weight.shape, BF16),
            pltpu.SemaphoreType.DMA((6,)),
        ],
    )(lane, *near(query, key, value, before, probs), *pieces, *far(out_weight))

    prefix, grad, local, phi, phit = after(prefix, grad, local, phi, phit)
    prefix = prefix.reshape(states)

    grad_state, mixed, grad_linear = kernel(
        mix_kernel,
        "mix",
        [NEAR] * 8,
        [HBM(states, BF16), VMEM((count, width), BF16), VMEM((count, width), BF16)],
    )(*near(prefix, phi, phit, local, attended, grad, cum), *far(norm_gain.reshape(1, width)))

    arrived = swap(grad_state.reshape(chunks))

    returned = lax.ppermute(edge_grad, "seq", [(i + 1, i) for i in range(peers - 1)])
    sums = kernel(
        project_kernel,
        "project",
        [SCALARS, NEAR, FAR],
        [HBM((count // ways, model), BF16)] * ways,
        8,
        [
            pltpu.VMEM((count, width), BF16),
            pltpu.VMEM(out_weight.shape, BF16),
            pltpu.SemaphoreType.DMA((ways,)),
        ],
    )(lane, *near(mixed), *far(out_weight))

    arrived, kept = after(arrived, sums[0])
    sums = [kept] + [shifted(sums[k], ways, k) for k in range(1, ways)]
    suffix = swap(chain(arrived, True))

    gq_t, gk_local, gv_local = kernel(
        intra_grad_kernel,
        "intra_grad",
        [NEAR] * 9,
        [
            HBM((HEADS * FEAT, TOK), BF16),
            VMEM((HEADS * FEAT, TOK), F32),
            VMEM((count, width), F32),
        ],
    )(
        fq_t, fk_t, *far(value_arg), *near(cum, cum_row), sel_q, sel_qt,
        *near(prefix, grad_linear),
    )
    layer_out = sum(p.astype(F32) for p in sums).astype(BF16)

    suffix, gk_local, gv_local, layer_out, returned = after(
        suffix, gk_local, gv_local, layer_out, returned
    )

    grad_key, grad_value, gfk_t = kernel(
        finish_kernel,
        "finish",
        [NEAR] * 11,
        [HBM((count, width), BF16), HBM((count, width), BF16), HBM((HEADS * FEAT, TOK), BF16)],
    )(
        fk_t, *near(faded, cum), sel_k, sel_kt,
        *near(suffix.reshape(states), gv_local, gk_local, win_key, win_value, returned),
    )
    return (layer_out, grad_query, grad_key, grad_value, gq_t.T, gfk_t.T)


def solution(mesh):
    return jax.shard_map(
        body,
        mesh=mesh,
        in_specs=(
            P("seq", "mp"),
            P("seq", "mp"),
            P("seq", "mp"),
            P("seq", "mp"),
            P("seq", "mp"),
            P("mp", "seq"),
            P("seq"),
            P("mp"),
            P("mp", None),
            P(("seq", "mp"), None),
        ),
        out_specs=(
            P(("seq", "mp"), None),
            P("seq", "mp"),
            P("seq", "mp"),
            P("seq", "mp"),
            P("seq", "mp"),
            P("seq", "mp"),
        ),
        check_vma=False,
    )
```

time: 140 us -> 115 us (0.82)
  local copies, waits for them, and re-layouts: 28.1 us -> 7.55 us
  Pallas kernels: 31.5 us -> 35.4 us
  waiting for transfers between devices: 15.2 us -> 12.2 us
  starting transfers between devices: 58.9 us -> 56.9 us
  matrix products: 1.66 us -> 0 us
    unnamed x88 -> x34, local copies, waits for them, and re-layouts: 21.1 us -> 7.55 us
    ppermute x6, waiting for transfers between devices: 11.6 us -> 0.02 us  [shifted(): return lax.ppermute(value, 'mp', [(i, (i + k) % ways) for i in range(ways)])]
    dynamic_update_slice x4 -> x0, local copies, waits for them, and re-layouts: 5.76 us -> none  [body(): lax.dynamic_update_slice(grad_rows, piece[None], ((lane - k) % ways, 0, 0))]
    all_to_all x4, waiting for transfers between devices: 3.6 us -> 8.49 us  [swap(): return lax.all_to_all(value, 'seq', split_axis=0, concat_axis=0, tiled=True)]
    pallas_call x9 -> x10, Pallas kernels: 31.5 us -> 35.4 us  [the longest x1 8.56 us: body(): kernel(window_grad_kernel, 'window_grad', [SCALARS] + [NEAR] * 5 + [ANYWH...]
    ppermute x1, waiting for transfers between devices: 0.01 us -> 2.23 us  [body(): before = lax.ppermute(edge, 'seq', [(i, i + 1) for i in range(peers - 1)])]
    dot_general x1 -> x0, matrix products: 1.66 us -> none  [body(): jnp.dot(mixed, out_weight, preferred_element_type=F32).astype(BF16)]
    ppermute x1, waiting for transfers between devices: 0.01 us -> 1.47 us  [body(): lax.ppermute(edge_grad, 'seq', [(i + 1, i) for i in range(peers - 1)])]
  transfers between devices with their start and end apart: 12 -> 12, of which waited for: 2 -> 4; matrix products, arithmetic and copies ran while one was open for 8% -> 2% of each run, Pallas kernels for 18% -> 21%
where the time goes in v1:
time: 115 us
  starting transfers between devices  56.9 us (49%)
  Pallas kernels  35.4 us (31%)
  waiting for transfers between devices  12.2 us (11%)
  local copies, waits for them, and re-layouts  7.55 us (7%)
  other arithmetic  1.79 us (2%)
    all_to_all x4, starting transfers between devices, swap(): return lax.all_to_all(value, 'seq', split_axis=0, concat_axis=0, tiled=True)  41.9 us
    pallas_call x1, Pallas kernels, body(): kernel(window_grad_kernel, 'window_grad', [SCALARS] + [NEAR] * 5 + [ANYWH...  8.56 us
    all_to_all x4, waiting for transfers between devices, swap(): return lax.all_to_all(value, 'seq', split_axis=0, concat_axis=0, tiled=True)  8.49 us
    ppermute x6, starting transfers between devices, shifted(): return lax.ppermute(value, 'mp', [(i, (i + k) % ways) for i in range(ways)])  8.26 us
    unnamed x34, local copies, waits for them, and re-layouts  7.55 us
    pallas_call x1, Pallas kernels, body(): kernel(window_kernel, 'window', [SCALARS] * 2 + [NEAR] * 4, [VMEM((count,...  5.74 us
    ppermute x1, starting transfers between devices, body(): before = lax.ppermute(edge, 'seq', [(i, i + 1) for i in range(peers - 1)])  4.37 us
    pallas_call x1, Pallas kernels, body(): kernel(local_state_kernel, 'local_state', [NEAR] * 3 + [FAR] * 3, [HBM(st...  3.97 us
  transfers between devices with their start and end apart: 12, of which 4 were waited for; matrix products, arithmetic and copies ran while one was open for 2% of the time, Pallas kernels for 21%

profile of v1, /device:TPU:1, one launch (start us, length us, event | category | flops | bytes accessed | tf_op | source)
XLA Modules:
  0.0 114.7 jit_solution(16010430691673326284)
XLA Ops:
  0.6 4.0 %local_state.1 = (bf16[1024,128]{1,0:T(8,128)(2,1)}, f32[256,4]{1,0:T(8,128)S(1)}, f32[4,1,256]{2,1,0:T(1,128)S(1)}, bf16[128,512]{1,0:T(8,128)(2,1)}, bf16[256,...) custom-call(bf16[64,256]{1,0:T(8,128)(2,1)} %bitcast.14, ...), custom_call_target="tpu_custom_call" | custom-call | tf_op jit(solution)/shard_map/local_state/pallas_call | solution.py:404
  4.6 13.2 %all-to-all-start = ((bf16[64,16,128]{2,1,0:T(8,128)(2,1)}), bf16[64,16,128]{2,1,0:T(8,128)(2,1)S(1)}, u32[]{:S(2)}, u32[]{:S(2)}) async-start(bf16[64,16,128]{2,1,0:T(8,128)(2,1)} %bitcast.18), calls=%async_computation | async-start | bytes 524288 | tf_op jit(solution)/shard_map/all_to_all | solution.py:367
  17.8 2.8 %collective-permute-start.2 = (bf16[64,2048]{1,0:T(8,128)(2,1)}, bf16[64,2048]{1,0:T(8,128)(2,1)S(1)}, u32[]{:S(2)}, u32[]{:S(2)}) collective-permute-start(bf16[64,2048]{1,0:T(8,128)(2,1)} %piece0), channel_id=1, source_target_pairs={{0,2},{1,3},{2,0},{3,1},{4,6},{5,7},{6,4},{7,5},{8,10},{9,11},{10,... | collective-permute-start | bytes 786440 | tf_op jit(solution)/shard_map/ppermute | solution.py:385
  20.9 2.4 %collective-permute-start.3 = (bf16[64,2048]{1,0:T(8,128)(2,1)}, bf16[64,2048]{1,0:T(8,128)(2,1)S(1)}, u32[]{:S(2)}, u32[]{:S(2)}) collective-permute-start(bf16[64,2048]{1,0:T(8,128)(2,1)} %piece0), channel_id=1, source_target_pairs={{0,3},{1,0},{2,1},{3,2},{4,7},{5,4},{6,5},{7,6},{8,11},{9,8},{10,9... | collective-permute-start | bytes 786440 | tf_op jit(solution)/shard_map/ppermute | solution.py:385
  23.3 4.4 %collective-permute-start = (bf16[128,512]{1,0:T(8,128)(2,1)}, bf16[128,512]{1,0:T(8,128)(2,1)S(1)}, u32[]{:S(2)}, u32[]{:S(2)}) collective-permute-start(bf16[128,512]{1,0:T(8,128)(2,1)} %get-tuple-element.62), channel_id=1, source_target_pairs={{0,4},{4,8},{8,12},{12,16},{16,20},{20,24},{24,28},{28,32},{32,36}... | collective-permute-start | bytes 393224 | tf_op jit(solution)/shard_map/ppermute | solution.py:424
  27.7 2.2 %collective-permute-done.before = bf16[128,512]{1,0:T(8,128)(2,1)S(1)} collective-permute-done((bf16[128,512]{1,0:T(8,128)(2,1)}, bf16[128,512]{1,0:T(8,128)(2,1)S(1)}, u32[]{:S(2)}, u32[]{:S(2)}) %collective-permute-start) | collective-permute-done | bytes 131104 | tf_op jit(solution)/shard_map/ppermute | solution.py:424
  30.6 5.7 %window.1 = (bf16[256,512]{1,0:T(8,128)(2,1)S(1)}, bf16[256,512]{1,0:T(8,128)(2,1)S(1)}) custom-call(s32[4]{0:T(128)S(1)} %copy-done.14, s32[1]{0:T(128)} %bitcast.2.first_col, bf16[256,512]{1,0:T(8,128)(2,1)S(1)} %get-tuple-element.59.query, bf16[256,512]{1,0:T(8,128)(2,1)S(1)} %get-tuple-element.60.key, bf16[256,512]{1,0:T(8,128)(2,1)S(1)} %get-tuple-element.61.value, ...), custom_call_target="tpu_custom_call" | custom-call | tf_op jit(solution)/shard_map/window/pallas_call | solution.py:428
  38.6 12.2 %all-to-all-start.1 = ((bf16[64,16,128]{2,1,0:T(8,128)(2,1)}), bf16[64,16,128]{2,1,0:T(8,128)(2,1)S(1)}, u32[]{:S(2)}, u32[]{:S(2)}) async-start(bf16[64,16,128]{2,1,0:T(8,128)(2,1)} %chain_fwd.1), calls=%async_computation.1 | async-start | bytes 524288 | tf_op jit(solution)/shard_map/all_to_all | solution.py:367
  50.9 2.2 %intra.1 = (f32[256,512]{1,0:T(8,128)S(1)}, bf16[256,1024]{1,0:T(8,128)(2,1)S(1)}, bf16[1024,256]{1,0:T(8,128)(2,1)S(1)}) custom-call(bf16[64,256]{1,0:T(8,128)(2,1)} %bitcast.20, bf16[64,256]{1,0:T(8,128)(2,1)} %bitcast.15, bf16[256,512]{1,0:T(8,128)(2,1)S(1)} %get-tuple-element.61.value, f32[256,4]{1,0:T(8,128)S(1)} %get-tuple-element.74.cum, ...), custom_call_target="tpu_custom_call" | custom-call | tf_op jit(solution)/shard_map/intra/pallas_call | solution.py:439
  54.1 0.9 copy-done.4
  56.0 8.6 %window_grad.1 = (bf16[256,512]{1,0:T(8,128)(2,1)S(1)}, bf16[256,512]{1,0:T(8,128)(2,1)}, bf16[256,512]{1,0:T(8,128)(2,1)}, bf16[256,512]{1,0:T(8,128)(2,1)}, bf16[128,512]{1,0:T(8,128)(2,1)}) custom-call(s32[1]{0:T(128)} %bitcast.4.place, bf16[256,512]{1,0:T(8,128)(2,1)S(1)} %get-tuple-element.59.query, bf16[256,512]{1,0:T(8,128)(2,1)S(1)} %get-tuple-element.60.key, ...), custom_call_target="tpu_custom_call" | custom-call | tf_op jit(solution)/shard_map/window_grad/pallas_call | solution.py:450
  65.3 0.9 copy-done.11
  67.2 2.4 %mix.1 = (bf16[1024,128]{1,0:T(8,128)(2,1)}, bf16[256,512]{1,0:T(8,128)(2,1)S(1)}, bf16[256,512]{1,0:T(8,128)(2,1)S(1)}) custom-call(bf16[1024,128]{1,0:T(8,128)(2,1)S(1)} %bitcast.11, bf16[256,1024]{1,0:T(8,128)(2,1)S(1)} %get-tuple-element.80.phi, bf16[1024,256]{1,0:T(8,128)(2,1)S(1)} %get-tuple-element.81.phit, f32[256,512]{1,0:T(8,128)S(1)} %get-tuple-element.82.local, ...), custom_call_target="tpu_custom_call" | custom-call | tf_op jit(solution)/shard_map/mix/pallas_call | solution.py:472
  69.5 10.5 %all-to-all-start.2 = ((bf16[64,16,128]{2,1,0:T(8,128)(2,1)}), bf16[64,16,128]{2,1,0:T(8,128)(2,1)S(1)}, u32[]{:S(2)}, u32[]{:S(2)}) async-start(bf16[64,16,128]{2,1,0:T(8,128)(2,1)} %bitcast.19), calls=%async_computation.2 | async-start | bytes 524288 | tf_op jit(solution)/shard_map/all_to_all | solution.py:367
  80.0 3.2 %project.1 = (bf16[64,2048]{1,0:T(8,128)(2,1)}, bf16[64,2048]{1,0:T(8,128)(2,1)}, bf16[64,2048]{1,0:T(8,128)(2,1)}, bf16[64,2048]{1,0:T(8,128)(2,1)}) custom-call(s32[1]{0:T(128)} %bitcast.4.place, bf16[256,512]{1,0:T(8,128)(2,1)S(1)} %get-tuple-element.86.mixed, bf16[512,2048]{1,0:T(8,128)(2,1)} %weight_far.3), custom_call_target="tpu_custom_call" | custom-call | tf_op jit(solution)/shard_map/project/pallas_call | solution.py:482
  84.2 1.8 %collective-permute-start.6 = (bf16[64,2048]{1,0:T(8,128)(2,1)}, bf16[64,2048]{1,0:T(8,128)(2,1)}, u32[]{:S(2)}, u32[]{:S(2)}) collective-permute-start(bf16[64,2048]{1,0:T(8,128)(2,1)} %get-tuple-element.95), channel_id=1, source_target_pairs={{0,3},{1,0},{2,1},{3,2},{4,7},{5,4},{6,5},{7,6},{8,11},{9,8},{10,9... | collective-permute-start | bytes 786440 | tf_op jit(solution)/shard_map/ppermute | solution.py:385
  86.0 6.0 %all-to-all-done.2.a = bf16[64,16,128]{2,1,0:T(8,128)(2,1)S(1)} async-done(((bf16[64,16,128]{2,1,0:T(8,128)(2,1)}), bf16[64,16,128]{2,1,0:T(8,128)(2,1)S(1)}, u32[]{:S(2)}, u32[]{:S(2)}) %all-to-all-start.2) | async-done | bytes 262176 | tf_op jit(solution)/shard_map/all_to_all | solution.py:367
  92.8 6.0 %all-to-all-start.3 = ((bf16[64,16,128]{2,1,0:T(8,128)(2,1)}), bf16[64,16,128]{2,1,0:T(8,128)(2,1)S(1)}, u32[]{:S(2)}, u32[]{:S(2)}) async-start(bf16[64,16,128]{2,1,0:T(8,128)(2,1)} %chain_back.1), calls=%async_computation.3 | async-start | bytes 524288 | tf_op jit(solution)/shard_map/all_to_all | solution.py:367
  98.9 2.4 %collective-permute-start.7 = (bf16[128,512]{1,0:T(8,128)(2,1)S(1)}, bf16[128,512]{1,0:T(8,128)(2,1)S(1)}, u32[]{:S(2)}, u32[]{:S(2)}) collective-permute-start(bf16[128,512]{1,0:T(8,128)(2,1)S(1)} %copy-done.16), channel_id=1, source_target_pairs={{4,0},{8,4},{12,8},{16,12},{20,16},{24,20},{28,24},{32,28},{36,32}... | collective-permute-start | bytes 393224 | tf_op jit(solution)/shard_map/ppermute | solution.py:481
  101.3 3.8 %intra_grad.1 = (bf16[64,256]{1,0:T(8,128)(2,1)}, f32[64,256]{1,0:T(8,128)S(1)}, f32[256,512]{1,0:T(8,128)S(1)}) custom-call(bf16[64,256]{1,0:T(8,128)(2,1)} %bitcast.21, bf16[64,256]{1,0:T(8,128)(2,1)} %bitcast.16, bf16[256,512]{1,0:T(8,128)(2,1)} %value.1, f32[256,4]{1,0:T(8,128)S(1)} %get-tuple-element.74.cum, ...), custom_call_target="tpu_custom_call" | custom-call | tf_op jit(solution)/shard_map/intra_grad/pallas_call | solution.py:499
  105.1 1.8 %add_convert_fusion = bf16[64,2048]{1,0:T(8,128)(2,1)} fusion(bf16[64,2048]{1,0:T(8,128)(2,1)} %collective-permute-done.6, bf16[64,2048]{1,0:T(8,128)(2,1)S(1)} %collective-permute-done.5, bf16[64,2048]{1,0:T(8,128)(2,1)S(1)} %collective-permute-done.4, bf16[64,2048]{1,0:T(8,128)(2,1)S(1)} %copy-done.15), kind=kLoop, calls=%fused_computation | loop fusion | flops 1048576 | bytes 1310720 | tf_op jit(solution)/shard_map/convert_element_type | solution.py:512
  106.9 1.5 %collective-permute-done.7.edge = bf16[128,512]{1,0:T(8,128)(2,1)S(1)} collective-permute-done((bf16[128,512]{1,0:T(8,128)(2,1)S(1)}, bf16[128,512]{1,0:T(8,128)(2,1)S(1)}, u32[]{:S(2)}, u32[]{:S(2)}) %collective-permute-start.7) | collective-permute-done | bytes 131104 | tf_op jit(solution)/shard_map/ppermute | solution.py:481
  108.4 2.5 %all-to-all-done.3 = bf16[64,16,128]{2,1,0:T(8,128)(2,1)S(1)} async-done(((bf16[64,16,128]{2,1,0:T(8,128)(2,1)}), bf16[64,16,128]{2,1,0:T(8,128)(2,1)S(1)}, u32[]{:S(2)}, u32[]{:S(2)}) %all-to-all-start.3) | async-done | bytes 262176 | tf_op jit(solution)/shard_map/all_to_all | solution.py:367
  110.9 3.8 %finish.1 = (bf16[256,512]{1,0:T(8,128)(2,1)}, bf16[256,512]{1,0:T(8,128)(2,1)}, bf16[64,256]{1,0:T(8,128)(2,1)}) custom-call(bf16[64,256]{1,0:T(8,128)(2,1)} %bitcast.17, bf16[256,512]{1,0:T(8,128)(2,1)S(1)} %copy-done.7, f32[256,4]{1,0:T(8,128)S(1)} %get-tuple-element.74.cum, bf16[512,16]{1,0:T(8,128)(2,1)} %constant.21.clone.sel, ...), custom_call_target="tpu_custom_call" | custom-call | tf_op jit(solution)/shard_map/finish/pallas_call | solution.py:518
  (45 shorter events, 8.7 us)
Async XLA Ops:
  0.6 52.5 %copy-start = (bf16[64,2048]{1,0:T(8,128)(2,1)S(1)}, bf16[64,2048]{1,0:T(8,128)(2,1)}, u32[]{:S(2)}) copy-start(bf16[64,2048]{1,0:T(8,128)(2,1)} %piece0) | copy-start | bytes 786436
  4.6 33.1 %all-to-all-start = ((bf16[64,16,128]{2,1,0:T(8,128)(2,1)}), bf16[64,16,128]{2,1,0:T(8,128)(2,1)S(1)}, u32[]{:S(2)}, u32[]{:S(2)}) async-start(bf16[64,16,128]{2,1,0:T(8,128)(2,1)} %bitcast.18), calls=%async_computation | async-start | bytes 524288 | tf_op jit(solution)/shard_map/all_to_all | solution.py:367
  17.8 19.9 %collective-permute-start.2 = (bf16[64,2048]{1,0:T(8,128)(2,1)}, bf16[64,2048]{1,0:T(8,128)(2,1)S(1)}, u32[]{:S(2)}, u32[]{:S(2)}) collective-permute-start(bf16[64,2048]{1,0:T(8,128)(2,1)} %piece0), channel_id=1, source_target_pairs={{0,2},{1,3},{2,0},{3,1},{4,6},{5,7},{6,4},{7,5},{8,10},{9,11},{10,... | collective-permute-start | bytes 786440 | tf_op jit(solution)/shard_map/ppermute | solution.py:385
  20.6 17.1 %collective-permute-start.1 = (bf16[64,2048]{1,0:T(8,128)(2,1)}, bf16[64,2048]{1,0:T(8,128)(2,1)S(1)}, u32[]{:S(2)}, u32[]{:S(2)}) collective-permute-start(bf16[64,2048]{1,0:T(8,128)(2,1)} %piece0), channel_id=1, source_target_pairs={{0,1},{1,2},{2,3},{3,0},{4,5},{5,6},{6,7},{7,4},{8,9},{9,10},{10,1... | collective-permute-start | bytes 786440 | tf_op jit(solution)/shard_map/ppermute | solution.py:385
  20.9 16.8 %collective-permute-start.3 = (bf16[64,2048]{1,0:T(8,128)(2,1)}, bf16[64,2048]{1,0:T(8,128)(2,1)S(1)}, u32[]{:S(2)}, u32[]{:S(2)}) collective-permute-start(bf16[64,2048]{1,0:T(8,128)(2,1)} %piece0), channel_id=1, source_target_pairs={{0,3},{1,0},{2,1},{3,2},{4,7},{5,4},{6,5},{7,6},{8,11},{9,8},{10,9... | collective-permute-start | bytes 786440 | tf_op jit(solution)/shard_map/ppermute | solution.py:385
  23.3 6.6 %collective-permute-start = (bf16[128,512]{1,0:T(8,128)(2,1)}, bf16[128,512]{1,0:T(8,128)(2,1)S(1)}, u32[]{:S(2)}, u32[]{:S(2)}) collective-permute-start(bf16[128,512]{1,0:T(8,128)(2,1)} %get-tuple-element.62), channel_id=1, source_target_pairs={{0,4},{4,8},{8,12},{12,16},{16,20},{20,24},{24,28},{28,32},{32,36}... | collective-permute-start | bytes 393224 | tf_op jit(solution)/shard_map/ppermute | solution.py:424
  37.7 13.2 %copy-start.1 = (bf16[64,2048]{1,0:T(8,128)(2,1)}, bf16[64,2048]{1,0:T(8,128)(2,1)S(1)}, u32[]{:S(2)}) copy-start(bf16[64,2048]{1,0:T(8,128)(2,1)S(1)} %collective-permute-done.1.piece1) | copy-start | bytes 786436
  37.7 13.2 %copy-start.3 = (bf16[64,2048]{1,0:T(8,128)(2,1)}, bf16[64,2048]{1,0:T(8,128)(2,1)S(1)}, u32[]{:S(2)}) copy-start(bf16[64,2048]{1,0:T(8,128)(2,1)S(1)} %collective-permute-done.3.piece3) | copy-start | bytes 786436
  38.6 26.6 %all-to-all-start.1 = ((bf16[64,16,128]{2,1,0:T(8,128)(2,1)}), bf16[64,16,128]{2,1,0:T(8,128)(2,1)S(1)}, u32[]{:S(2)}, u32[]{:S(2)}) async-start(bf16[64,16,128]{2,1,0:T(8,128)(2,1)} %chain_fwd.1), calls=%async_computation.1 | async-start | bytes 524288 | tf_op jit(solution)/shard_map/all_to_all | solution.py:367
  53.1 1.0 copy-start.2
  54.1 0.9 copy-start.4
  55.0 0.9 copy-start.6
  65.3 1.0 copy-start.11
  69.5 29.3 %copy-start.16 = (bf16[128,512]{1,0:T(8,128)(2,1)S(1)}, bf16[128,512]{1,0:T(8,128)(2,1)}, u32[]{:S(2)}) copy-start(bf16[128,512]{1,0:T(8,128)(2,1)} %get-tuple-element.96) | copy-start | bytes 393220
  69.5 22.5 %all-to-all-start.2 = ((bf16[64,16,128]{2,1,0:T(8,128)(2,1)}), bf16[64,16,128]{2,1,0:T(8,128)(2,1)S(1)}, u32[]{:S(2)}, u32[]{:S(2)}) async-start(bf16[64,16,128]{2,1,0:T(8,128)(2,1)} %bitcast.19), calls=%async_computation.2 | async-start | bytes 524288 | tf_op jit(solution)/shard_map/all_to_all | solution.py:367
  83.2 21.9 %copy-start.15 = (bf16[64,2048]{1,0:T(8,128)(2,1)S(1)}, bf16[64,2048]{1,0:T(8,128)(2,1)}, u32[]{:S(2)}) copy-start(bf16[64,2048]{1,0:T(8,128)(2,1)} %get-tuple-element.92) | copy-start | bytes 786436
  83.2 27.7 %copy-start.7 = (bf16[256,512]{1,0:T(8,128)(2,1)S(1)}, bf16[256,512]{1,0:T(8,128)(2,1)}, u32[]{:S(2)}) copy-start(bf16[256,512]{1,0:T(8,128)(2,1)} %get-tuple-element.99.faded) | copy-start | bytes 786436
  83.2 27.6 %copy-start.8 = (bf16[256,512]{1,0:T(8,128)(2,1)S(1)}, bf16[256,512]{1,0:T(8,128)(2,1)}, u32[]{:S(2)}) copy-start(bf16[256,512]{1,0:T(8,128)(2,1)} %get-tuple-element.103.window_key) | copy-start | bytes 786436
  83.2 27.6 %copy-start.9 = (bf16[256,512]{1,0:T(8,128)(2,1)S(1)}, bf16[256,512]{1,0:T(8,128)(2,1)}, u32[]{:S(2)}) copy-start(bf16[256,512]{1,0:T(8,128)(2,1)} %get-tuple-element.104.window_value) | copy-start | bytes 786436
  83.3 21.8 %collective-permute-start.4 = (bf16[64,2048]{1,0:T(8,128)(2,1)}, bf16[64,2048]{1,0:T(8,128)(2,1)S(1)}, u32[]{:S(2)}, u32[]{:S(2)}) collective-permute-start(bf16[64,2048]{1,0:T(8,128)(2,1)} %get-tuple-element.93), channel_id=1, source_target_pairs={{0,1},{1,2},{2,3},{3,0},{4,5},{5,6},{6,7},{7,4},{8,9},{9,10},{10,1... | collective-permute-start | bytes 786440 | tf_op jit(solution)/shard_map/ppermute | solution.py:385
  83.3 21.8 %collective-permute-start.5 = (bf16[64,2048]{1,0:T(8,128)(2,1)}, bf16[64,2048]{1,0:T(8,128)(2,1)S(1)}, u32[]{:S(2)}, u32[]{:S(2)}) collective-permute-start(bf16[64,2048]{1,0:T(8,128)(2,1)} %get-tuple-element.94), channel_id=1, source_target_pairs={{0,2},{1,3},{2,0},{3,1},{4,6},{5,7},{6,4},{7,5},{8,10},{9,11},{10,... | collective-permute-start | bytes 786440 | tf_op jit(solution)/shard_map/ppermute | solution.py:385
  84.2 20.9 %collective-permute-start.6 = (bf16[64,2048]{1,0:T(8,128)(2,1)}, bf16[64,2048]{1,0:T(8,128)(2,1)}, u32[]{:S(2)}, u32[]{:S(2)}) collective-permute-start(bf16[64,2048]{1,0:T(8,128)(2,1)} %get-tuple-element.95), channel_id=1, source_target_pairs={{0,3},{1,0},{2,1},{3,2},{4,7},{5,4},{6,5},{7,6},{8,11},{9,8},{10,9... | collective-permute-start | bytes 786440 | tf_op jit(solution)/shard_map/ppermute | solution.py:385
  92.8 18.0 %all-to-all-start.3 = ((bf16[64,16,128]{2,1,0:T(8,128)(2,1)}), bf16[64,16,128]{2,1,0:T(8,128)(2,1)S(1)}, u32[]{:S(2)}, u32[]{:S(2)}) async-start(bf16[64,16,128]{2,1,0:T(8,128)(2,1)} %chain_back.1), calls=%async_computation.3 | async-start | bytes 524288 | tf_op jit(solution)/shard_map/all_to_all | solution.py:367
  98.9 9.5 %collective-permute-start.7 = (bf16[128,512]{1,0:T(8,128)(2,1)S(1)}, bf16[128,512]{1,0:T(8,128)(2,1)S(1)}, u32[]{:S(2)}, u32[]{:S(2)}) collective-permute-start(bf16[128,512]{1,0:T(8,128)(2,1)S(1)} %copy-done.16), channel_id=1, source_target_pairs={{4,0},{8,4},{12,8},{16,12},{20,16},{24,20},{28,24},{32,28},{36,32}... | collective-permute-start | bytes 393224 | tf_op jit(solution)/shard_map/ppermute | solution.py:481
  (5 other events, 3.7 us)

commit v2 on v1

--- a/solution.py
+++ b/solution.py
@@ -161,7 +161,7 @@
     return array[(b - 1) * WINDOW : (b + 1) * WINDOW, :]
 
 
-def intra_kernel(fq_t, fk_t, value, cum, cum_row, sel, sel_t, local_out, phi_out, phit_out):
+def intra_kernel(fq_t, fk_t, value, cum, cum_row, sel_t, local_out, phi_out):
     for h in range(HEADS):
         feats = fq_t[head_feats(h), :]
         _, _, weights = intra_weights(
@@ -170,8 +170,30 @@
         local_out[:, head_cols(h)] = mm(weights.astype(BF16), value[:, head_cols(h)], NN)
         left, right = factors_cols(feats, sel_t[...], 1 / 16)
         phi_out[:, head_rows(h)] = (left * right).astype(BF16)
-        left, right = factors_rows(feats, sel[...], 1 / 16)
-        phit_out[head_rows(h), :] = (left * right).astype(BF16)
+
+
+def stacked(parts):
+    return jnp.concatenate(parts, axis=0)
+
+
+def grad_mixed_kernel(
+    place, piece0, piece1, piece2, piece3, weight_far, grad_out, rows, weight, sems
+):
+    pieces = (piece0, piece1, piece2, piece3)
+    half = weight.shape[0] // 2
+    copies = []
+    for k, piece in enumerate(pieces):
+        at = ((place[0] + (len(pieces) - k)) % len(pieces)) * WINDOW
+        to = rows.at[pl.ds(pl.multiple_of(at, WINDOW), WINDOW), :]
+        copies.append(pltpu.make_async_copy(piece, to, sems.at[k]))
+    copies.append(pltpu.make_async_copy(weight_far, weight, sems.at[4]))
+    for copy in copies:
+        copy.start()
+    for copy in copies:
+        copy.wait()
+    for i in range(2):
+        part = slice(i * half, (i + 1) * half)
+        grad_out[:, part] = mm(rows[...], weight[part, :], NT).astype(BF16)
 
 
 def window_kernel(band, first_col, query, key, value, before, attended_out, probs_out):
@@ -183,74 +205,82 @@
         allowed = (back >= 0) & (back < band[b])
         if b == 0:
             allowed = allowed & (col >= first_col[0])
+        scores = []
         for h in range(HEADS):
             cols = head_cols(h)
             keys = block_pair(before[:WINDOW, cols], key.at[:, cols], b)
+            scores.append(jnp.where(allowed, mm(query[here, cols], keys, NT) * SCALE, NEG))
+        scores = stacked(scores)
+        expo = jnp.exp(scores - jnp.max(scores, axis=-1, keepdims=True))
+        probs = (expo * (1.0 / jnp.sum(expo, axis=-1, keepdims=True))).astype(BF16)
+        for h in range(HEADS):
+            cols = head_cols(h)
+            mine = probs[h * WINDOW : (h + 1) * WINDOW, :]
             values = block_pair(before[WINDOW:, cols], value.at[:, cols], b)
-            scores = mm(query[here, cols], keys, NT) * SCALE
-            scores = jnp.where(allowed, scores, NEG)
-            expo = jnp.exp(scores - jnp.max(scores, axis=-1, keepdims=True))
-            probs = expo / jnp.sum(expo, axis=-1, keepdims=True)
-            probs16 = probs.astype(BF16)
-            probs_out[here, cols] = probs16
-            attended_out[here, cols] = mm(probs16, values, NN).astype(BF16)
-
-
-def window_grad_kernel(
-    place, query, key, value, before, probs, piece0, piece1, piece2, piece3, weight_far,
-    grad_out, gq_out, gk_out, gv_out, edge_out, rows, weight, sems
-):
-    pieces = (piece0, piece1, piece2, piece3)
-    half = weight.shape[0] // 2
-    copies = []
-    for k, piece in enumerate(pieces):
-        at = ((place[0] + (len(pieces) - k)) % len(pieces)) * WINDOW
-        to = rows.at[pl.ds(pl.multiple_of(at, WINDOW), WINDOW), :]
-        copies.append(pltpu.make_async_copy(piece, to, sems.at[k]))
-    for i in range(2):
-        part = slice(i * half, (i + 1) * half)
-        copies.append(
-            pltpu.make_async_copy(weight_far.at[part, :], weight.at[part, :], sems.at[4 + i])
+            probs_out[here, cols] = mine
+            attended_out[here, cols] = mm(mine, values, NN).astype(BF16)
+
+
+def score_grads(probs32, grad_probs):
+    grad_probs = grad_probs.astype(BF16).astype(F32)
+    along = jnp.sum(probs32 * grad_probs, axis=-1, keepdims=True)
+    return (probs32 * (grad_probs - along) * SCALE).astype(BF16)
+
+
+def edge_grad_kernel(query, value, before, probs, grad, edge_out):
+    grads = [grad[:WINDOW, head_cols(h)] for h in range(HEADS)]
+    parts = []
+    for h in range(HEADS):
+        cols = head_cols(h)
+        values = block_pair(before[WINDOW:, cols], value.at[:, cols], 0)
+        parts.append(mm(grads[h], values, NT))
+    probs16 = stacked([probs[:WINDOW, head_cols(h)] for h in range(HEADS)])
+    grad_scores = score_grads(probs16.astype(F32), stacked(parts))
+    for h in range(HEADS):
+        cols = head_cols(h)
+        mine = slice(h * WINDOW, (h + 1) * WINDOW)
+        key_part = mm(grad_scores[mine, :], query[:WINDOW, cols], TN)
+        value_part = mm(probs16[mine, :], grads[h], TN)
+        edge_out[:WINDOW, cols] = key_part[:WINDOW, :].astype(BF16)
+        edge_out[WINDOW:, cols] = value_part[:WINDOW, :].astype(BF16)
+
+
+def window_grad_kernel(query, key, value, before, probs, grad, gq_out, gk_out, gv_out):
+    blocks = TOK // WINDOW
+    for h in range(HEADS):
+        cols = head_cols(h)
+        keys = [block_pair(before[:WINDOW, cols], key.at[:, cols], b) for b in range(blocks)]
+        heres = [slice(b * WINDOW, (b + 1) * WINDOW) for b in range(blocks)]
+        grad_probs = stacked(
+            [
+                mm(
+                    grad[heres[b], cols],
+                    block_pair(before[WINDOW:, cols], value.at[:, cols], b),
+                    NT,
+                )
+                for b in range(blocks)
+            ]
         )
-    for copy in copies:
-        copy.start()
-    for copy in copies[:5]:
-        copy.wait()
-    for h in range(HEADS):
-        cols = head_cols(h)
-        if h % 2 == 0:
-            if h > 0:
-                copies[5].wait()
-            pair = slice(h * SIZE, (h + 2) * SIZE)
-            grad16 = mm(rows[...], weight[pair, :], NT).astype(BF16)
-            grad_out[:, pair] = grad16
-        mine = head_cols(h % 2)
+        grad_scores = score_grads(probs[:, cols].astype(F32), grad_probs)
         key_parts = []
         value_parts = []
-        for b in range(TOK // WINDOW):
-            here = slice(b * WINDOW, (b + 1) * WINDOW)
-            keys = block_pair(before[:WINDOW, cols], key.at[:, cols], b)
-            values = block_pair(before[WINDOW:, cols], value.at[:, cols], b)
-            probs16 = probs[here, cols]
-            probs32 = probs16.astype(F32)
-            grad_here = grad16[here, mine]
-            grad_probs = mm(grad_here, values, NT).astype(BF16).astype(F32)
-            along = jnp.sum(probs32 * grad_probs, axis=-1, keepdims=True)
-            grad_scores = (probs32 * (grad_probs - along) * SCALE).astype(BF16)
-            gq_out[here, cols] = mm(grad_scores, keys, NN).astype(BF16)
-            key_parts.append(mm(grad_scores, query[here, cols], TN).astype(BF16))
-            value_parts.append(mm(probs16, grad_here, TN).astype(BF16))
-        for at, parts, out in ((0, key_parts, gk_out), (WINDOW, value_parts, gv_out)):
-            edge_out[at : at + WINDOW, cols] = parts[0][:WINDOW, :]
-            for b in range(TOK // WINDOW):
+        for b in range(blocks):
+            here = heres[b]
+            mine = grad_scores[here, :]
+            gq_out[here, cols] = mm(mine, keys[b], NN).astype(BF16)
+            key_parts.append(mm(mine, query[here, cols], TN).astype(BF16))
+            value_parts.append(mm(probs[here, cols], grad[here, cols], TN).astype(BF16))
+        for parts, out in ((key_parts, gk_out), (value_parts, gv_out)):
+            for b in range(blocks):
                 own = parts[b][WINDOW:, :]
-                if b + 1 < TOK // WINDOW:
+                if b + 1 < blocks:
                     own = own + parts[b + 1][:WINDOW, :]
-                out[b * WINDOW : (b + 1) * WINDOW, cols] = own
+                out[heres[b], cols] = own
 
 
 def mix_kernel(
-    state, phi, phit, local, attended, grad, cum, gain, grad_state_out, mixed_out, grad_linear_out
+    state, phi, fq_t, sel, local, attended, grad, cum, gain, grad_state_out, mixed_out,
+    grad_linear_out
 ):
     for h in range(HEADS):
         cols = head_cols(h)
@@ -259,12 +289,16 @@
         linear = local[:, cols] + fade * mm(phi[:, head_rows(h)], state[head_rows(h), :], NN)
         scale = lax.rsqrt(jnp.mean(linear * linear, axis=-1, keepdims=True) + EPS)
         gains = gain[:, cols]
-        mixed_out[:, cols] = (attended[:, cols].astype(F32) + linear * scale * gains).astype(BF16)
+        mixed_out[:, cols] = (
+            attended[:, cols].astype(F32) + linear * scale * gains
+        ).astype(BF16)
         scaled = grad[:, cols].astype(F32) * gains
         along = jnp.mean(scaled * linear, axis=-1, keepdims=True)
         grad_linear = scale * scaled - linear * (scale * scale * scale * along)
         grad_linear_out[:, cols] = grad_linear.astype(BF16)
-        grad_state = mm(phit[head_rows(h), :], (grad_linear * fade).astype(BF16), NN)
+        left, right = factors_rows(fq_t[head_feats(h), :], sel[...], 1 / 16)
+        phi_t = (left * right).astype(BF16)
+        grad_state = mm(phi_t, (grad_linear * fade).astype(BF16), NN)
         total = steps[TOK - 1 : TOK, :]
         grad_state_out[head_rows(h), :] = with_total(grad_state, total).astype(BF16)
 
@@ -290,7 +324,8 @@
 
 
 def intra_grad_kernel(
-    fq_t, fk_t, value, cum, cum_row, sel, sel_t, state, grad_linear, gq_out, gk_out, gv_out
+    fq_t, fk_t, value, cum, cum_row, sel, sel_t, sel_kt, state, grad_linear,
+    gq_out, gk_out, gv_out, phi_out
 ):
     for h in range(HEADS):
         cols = head_cols(h)
@@ -306,10 +341,12 @@
         left, right = factors_rows(fq, sel[...], 1 / 16)
         gq = mm(fk, grad_inner, NT) + feature_grad(grad_phi, left, right, sel_t[...])
         gq_out[head_feats(h), :] = gq.astype(BF16)
+        left, right = factors_cols(fk, sel_kt[...], 1.0)
+        phi_out[:, head_rows(h)] = (left * right).astype(BF16)
 
 
 def finish_kernel(
-    fk_t, faded, cum, sel, sel_t, suffix, gv_local, gk_local, window_key, window_value, edge,
+    fk_t, phi, faded, cum, sel, sel_t, suffix, gv_local, gk_local, window_key, window_value, edge,
     gk_out, gv_out, gfk_out
 ):
     last = TOK - WINDOW
@@ -320,8 +357,7 @@
         fk = fk_t[head_feats(h), :]
         steps = cum[:, h : h + 1]
         fade = jnp.exp(steps[TOK - 1 : TOK, :] - steps)
-        left, right = factors_cols(fk, sel_t[...], 1.0)
-        carried = mm((left * right).astype(BF16), suffix[head_rows(h), :], NN) * fade
+        carried = mm(phi[:, head_rows(h)], suffix[head_rows(h), :], NN) * fade
         gv = (gv_local[:, cols] + carried).astype(BF16)
         gv_out[:last, cols] = window_value[:last, cols] + gv[:last, :]
         gv_out[last:, cols] = (window_value[last:, cols] + edge[WINDOW:, cols]) + gv[last:, :]
@@ -332,6 +368,7 @@
 
 
 HBM = pltpu.HBM
+EARLY = (2,)
 VMEM = pltpu.VMEM
 NEAR = pl.BlockSpec(memory_space=pltpu.VMEM)
 FAR = pl.BlockSpec(memory_space=pltpu.HBM)
@@ -344,7 +381,7 @@
 
 
 def near(*values):
-    return [pltpu.with_memory_space_constraint(v, pltpu.VMEM) for v in values]
+    return [pltpu.with_memory_space_constraint(jnp.asarray(v), pltpu.VMEM) for v in values]
 
 
 def far(*values):
@@ -400,7 +437,7 @@
     states = (HEADS * ROWS, SIZE)
     model = grad_out.shape[1]
 
-    value_arg = value
+    value_arg, args = (value, (query, key, value))
     state, cum, cum_row, edge, faded, value, key, query = kernel(
         local_state_kernel,
         "local_state",
@@ -424,61 +461,54 @@
     before = lax.ppermute(edge, "seq", [(i, i + 1) for i in range(peers - 1)])
     pieces = [grad_out] + [shifted(grad_out, ways, k) for k in range(1, ways)]
 
+    arrived, before, *early = after(arrived, before, *(pieces[k] for k in EARLY))
+    for k, piece in zip(EARLY, early):
+        pieces[k] = piece
+    chained, before, fq_late = after(chain(arrived, False), before, feat_query.T)
+    prefix = swap(chained)
+
+    local, phi = kernel(
+        intra_kernel,
+        "intra",
+        [NEAR] * 6,
+        [VMEM((count, width), F32), VMEM((TOK, HEADS * ROWS), BF16)],
+    )(*far(fq_late), fk_t, *near(value, cum, cum_row), sel_qt)
+
     first_col = jnp.where(place == 0, WINDOW, 0).astype(jnp.int32)[None]
     attended, probs = kernel(
         window_kernel,
         "window",
         [SCALARS] * 2 + [NEAR] * 4,
-        [VMEM((count, width), BF16), VMEM((count, width), BF16)],
+        [VMEM((count, width), BF16)] * 2,
     )(band_width, first_col, *near(query, key, value, before))
-
-    arrived, attended, probs, *pieces = after(arrived, attended, probs, *pieces)
-    chained, fq_late = after(chain(arrived, False), feat_query.T)
-    prefix = swap(chained)
-
-    local, phi, phit = kernel(
-        intra_kernel,
-        "intra",
-        [NEAR] * 7,
-        [
-            VMEM((count, width), F32),
-            VMEM((TOK, HEADS * ROWS), BF16),
-            VMEM((HEADS * ROWS, TOK), BF16),
-        ],
-    )(*far(fq_late), fk_t, *near(value, cum, cum_row), sel_q, sel_qt)
-
-    grad, grad_query, win_key, win_value, edge_grad = kernel(
-        window_grad_kernel,
-        "window_grad",
-        [SCALARS] + [NEAR] * 5 + [ANYWHERE] * 4 + [FAR],
-        [
-            VMEM((count, width), BF16),
-            HBM((count, width), BF16),
-            HBM((count, width), BF16),
-            HBM((count, width), BF16),
-            HBM((2 * WINDOW, width), BF16),
-        ],
+    grad = kernel(
+        grad_mixed_kernel,
+        "grad_mixed",
+        [SCALARS] + [FAR] * 5,
+        [VMEM((count, width), BF16)],
         12,
         [
             pltpu.VMEM((count, model), BF16),
             pltpu.VMEM(out_weight.shape, BF16),
-            pltpu.SemaphoreType.DMA((6,)),
+            pltpu.SemaphoreType.DMA((5,)),
         ],
-    )(lane, *near(query, key, value, before, probs), *pieces, *far(out_weight))
-
-    prefix, grad, local, phi, phit = after(prefix, grad, local, phi, phit)
+    )(lane, *far(*pieces, out_weight))[0]
+
+    prefix, attended, probs, grad, local, phi = after(
+        prefix, attended, probs, grad, local, phi
+    )
     prefix = prefix.reshape(states)
 
     grad_state, mixed, grad_linear = kernel(
         mix_kernel,
         "mix",
-        [NEAR] * 8,
+        [NEAR] * 9,
         [HBM(states, BF16), VMEM((count, width), BF16), VMEM((count, width), BF16)],
-    )(*near(prefix, phi, phit, local, attended, grad, cum), *far(norm_gain.reshape(1, width)))
-
+    )(*near(prefix, phi, feat_query.T, SEL_Q, local, attended, grad, cum, norm_gain.reshape(1, width)))
+
+    grad_state, probs = after(grad_state, probs)
     arrived = swap(grad_state.reshape(chunks))
 
-    returned = lax.ppermute(edge_grad, "seq", [(i + 1, i) for i in range(peers - 1)])
     sums = kernel(
         project_kernel,
         "project",
@@ -494,34 +524,51 @@
 
     arrived, kept = after(arrived, sums[0])
     sums = [kept] + [shifted(sums[k], ways, k) for k in range(1, ways)]
-    suffix = swap(chain(arrived, True))
-
-    gq_t, gk_local, gv_local = kernel(
+    chained, probs = after(chain(arrived, True), probs)
+    suffix = swap(chained)
+
+    edge_grad = kernel(
+        edge_grad_kernel,
+        "edge_grad",
+        [NEAR] * 5,
+        [HBM((2 * WINDOW, width), BF16)],
+    )(*far(args[0], args[2]), *near(before, probs, grad))[0]
+    returned = lax.ppermute(edge_grad, "seq", [(i + 1, i) for i in range(peers - 1)])
+    edge_grad, probs = after(edge_grad, probs)
+    grad_query, win_key, win_value = kernel(
+        window_grad_kernel,
+        "window_grad",
+        [NEAR] * 6,
+        [HBM((count, width), BF16), VMEM((count, width), BF16), VMEM((count, width), BF16)],
+    )(*far(*args), *near(before, probs, grad))
+
+    gq_t, gk_local, gv_local, phi_k = kernel(
         intra_grad_kernel,
         "intra_grad",
-        [NEAR] * 9,
+        [NEAR] * 10,
         [
             HBM((HEADS * FEAT, TOK), BF16),
             VMEM((HEADS * FEAT, TOK), F32),
             VMEM((count, width), F32),
+            VMEM((TOK, HEADS * ROWS), BF16),
         ],
     )(
-        fq_t, fk_t, *far(value_arg), *near(cum, cum_row), sel_q, sel_qt,
+        fq_t, fk_t, *far(value_arg), *near(cum, cum_row), sel_q, sel_qt, sel_kt,
         *near(prefix, grad_linear),
     )
     layer_out = sum(p.astype(F32) for p in sums).astype(BF16)
 
-    suffix, gk_local, gv_local, layer_out, returned = after(
-        suffix, gk_local, gv_local, layer_out, returned
+    suffix, gk_local, gv_local, phi_k, layer_out, returned, win_key, win_value = after(
+        suffix, gk_local, gv_local, phi_k, layer_out, returned, win_key, win_value
     )
 
     grad_key, grad_value, gfk_t = kernel(
         finish_kernel,
         "finish",
-        [NEAR] * 11,
+        [NEAR] * 12,
         [HBM((count, width), BF16), HBM((count, width), BF16), HBM((HEADS * FEAT, TOK), BF16)],
     )(
-        fk_t, *near(faded, cum), sel_k, sel_kt,
+        *near(feat_key.T, phi_k, faded, cum, SEL_K, SEL_K_T),
         *near(suffix.reshape(states), gv_local, gk_local, win_key, win_value, returned),
     )
     return (layer_out, grad_query, grad_key, grad_value, gq_t.T, gfk_t.T)

time: 115 us -> 103 us (0.90); the launches traced: 115 us -> 101 us
  local copies, waits for them, and re-layouts: 7.55 us -> 0.06 us
  Pallas kernels: 35.4 us -> 29.9 us
  starting transfers between devices: 56.9 us -> 55.2 us
    unnamed x34 -> x22, local copies, waits for them, and re-layouts: 7.55 us -> 0.06 us
    pallas_call x1, Pallas kernels: 5.74 us -> 2.18 us  [body(): kernel(window_kernel, 'window', [SCALARS] * 2 + [NEAR] * 4, [VMEM((count,...]
    all_to_all x4, starting transfers between devices: 41.9 us -> 39.5 us  [swap(): return lax.all_to_all(value, 'seq', split_axis=0, concat_axis=0, tiled=True)]
    ppermute x6, waiting for transfers between devices: 0.02 us -> 2.07 us  [shifted(): return lax.ppermute(value, 'mp', [(i, (i + k) % ways) for i in range(ways)])]
    pallas_call x5 -> x7, Pallas kernels: 20.8 us -> 18.8 us  [the longest x1 3.94 us: body(): kernel(intra_grad_kernel, 'intra_grad', [NEAR] * 10, [HBM((HEADS * FEAT,...]
    ppermute x1, waiting for transfers between devices: 1.47 us -> 0.01 us  [body(): lax.ppermute(edge_grad, 'seq', [(i + 1, i) for i in range(peers - 1)])]
    ppermute x6, starting transfers between devices: 8.26 us -> 9.53 us  [shifted(): return lax.ppermute(value, 'mp', [(i, (i + k) % ways) for i in range(ways)])]
  transfers between devices with their start and end apart: 12 -> 12, of which waited for: 4 -> 5; matrix products, arithmetic and copies ran while one was open for 2% -> 2% of each run, Pallas kernels for 21% -> 20%
where the time goes in v2:
time: 103 us; the launch traced here: 101 us
  starting transfers between devices  55.2 us (54%)
  Pallas kernels  29.9 us (29%)
  waiting for transfers between devices  12.7 us (12%)
  other arithmetic  1.91 us (2%)
    all_to_all x4, starting transfers between devices, swap(): return lax.all_to_all(value, 'seq', split_axis=0, concat_axis=0, tiled=True)  39.5 us
    ppermute x6, starting transfers between devices, shifted(): return lax.ppermute(value, 'mp', [(i, (i + k) % ways) for i in range(ways)])  9.53 us
    all_to_all x4, waiting for transfers between devices, swap(): return lax.all_to_all(value, 'seq', split_axis=0, concat_axis=0, tiled=True)  8.03 us
    pallas_call x1, Pallas kernels, body(): kernel(local_state_kernel, 'local_state', [NEAR] * 3 + [FAR] * 3, [HBM(st...  3.97 us
    pallas_call x1, Pallas kernels, body(): kernel(intra_grad_kernel, 'intra_grad', [NEAR] * 10, [HBM((HEADS * FEAT,...  3.94 us
    ppermute x1, starting transfers between devices, body(): before = lax.ppermute(edge, 'seq', [(i, i + 1) for i in range(peers - 1)])  3.81 us
    pallas_call x1, Pallas kernels, body(): kernel(window_grad_kernel, 'window_grad', [NEAR] * 6, [HBM((count, width)...  3.56 us
    pallas_call x1, Pallas kernels, body(): kernel(project_kernel, 'project', [SCALARS, NEAR, FAR], [HBM((count // wa...  3.21 us
  transfers between devices with their start and end apart: 12, of which 5 were waited for; matrix products, arithmetic and copies ran while one was open for 2% of the time, Pallas kernels for 20%

profile of v2, /device:TPU:1, one launch (start us, length us, event | category | flops | bytes accessed | tf_op | source)
XLA Modules:
  0.0 100.5 jit_solution(16688077901197655337)
XLA Ops:
  0.7 4.0 %local_state.1 = (bf16[1024,128]{1,0:T(8,128)(2,1)}, f32[256,4]{1,0:T(8,128)S(1)}, f32[4,1,256]{2,1,0:T(1,128)S(1)}, bf16[128,512]{1,0:T(8,128)(2,1)}, bf16[256,...) custom-call(bf16[64,256]{1,0:T(8,128)(2,1)} %bitcast.14, ...), custom_call_target="tpu_custom_call" | custom-call | tf_op jit(solution)/shard_map/local_state/pallas_call | solution.py:441
  4.6 13.2 %all-to-all-start = ((bf16[64,16,128]{2,1,0:T(8,128)(2,1)}), bf16[64,16,128]{2,1,0:T(8,128)(2,1)S(1)}, u32[]{:S(2)}, u32[]{:S(2)}) async-start(bf16[64,16,128]{2,1,0:T(8,128)(2,1)} %bitcast.23), calls=%async_computation | async-start | bytes 524288 | tf_op jit(solution)/shard_map/all_to_all | solution.py:404
  17.8 2.8 %collective-permute-start.1 = (bf16[64,2048]{1,0:T(8,128)(2,1)}, bf16[64,2048]{1,0:T(8,128)(2,1)S(1)}, u32[]{:S(2)}, u32[]{:S(2)}) collective-permute-start(bf16[64,2048]{1,0:T(8,128)(2,1)} %piece0.1), channel_id=1, source_target_pairs={{0,2},{1,3},{2,0},{3,1},{4,6},{5,7},{6,4},{7,5},{8,10},{9,11},{10,... | collective-permute-start | bytes 786440 | tf_op jit(solution)/shard_map/ppermute | solution.py:422
  20.6 3.8 %collective-permute-start = (bf16[128,512]{1,0:T(8,128)(2,1)}, bf16[128,512]{1,0:T(8,128)(2,1)S(1)}, u32[]{:S(2)}, u32[]{:S(2)}) collective-permute-start(bf16[128,512]{1,0:T(8,128)(2,1)} %get-tuple-element.63), channel_id=1, source_target_pairs={{0,4},{4,8},{8,12},{12,16},{16,20},{20,24},{24,28},{28,32},{32,36}... | collective-permute-start | bytes 393224 | tf_op jit(solution)/shard_map/ppermute | solution.py:461
  24.4 2.6 %collective-permute-done.before = bf16[128,512]{1,0:T(8,128)(2,1)S(1)} collective-permute-done((bf16[128,512]{1,0:T(8,128)(2,1)}, bf16[128,512]{1,0:T(8,128)(2,1)S(1)}, u32[]{:S(2)}, u32[]{:S(2)}) %collective-permute-start) | collective-permute-done | bytes 131104 | tf_op jit(solution)/shard_map/ppermute | solution.py:461
  27.0 2.8 %all-to-all-done.a = bf16[64,16,128]{2,1,0:T(8,128)(2,1)S(1)} async-done(((bf16[64,16,128]{2,1,0:T(8,128)(2,1)}), bf16[64,16,128]{2,1,0:T(8,128)(2,1)S(1)}, u32[]{:S(2)}, u32[]{:S(2)}) %all-to-all-start) | async-done | bytes 262176 | tf_op jit(solution)/shard_map/all_to_all | solution.py:404
  30.7 9.1 %all-to-all-start.1 = ((bf16[64,16,128]{2,1,0:T(8,128)(2,1)}), bf16[64,16,128]{2,1,0:T(8,128)(2,1)S(1)}, u32[]{:S(2)}, u32[]{:S(2)}) async-start(bf16[64,16,128]{2,1,0:T(8,128)(2,1)} %chain_fwd.1), calls=%async_computation.1 | async-start | bytes 524288 | tf_op jit(solution)/shard_map/all_to_all | solution.py:404
  40.4 2.1 %collective-permute-start.3 = (bf16[64,2048]{1,0:T(8,128)(2,1)S(1)}, bf16[64,2048]{1,0:T(8,128)(2,1)}, u32[]{:S(2)}, u32[]{:S(2)}) collective-permute-start(bf16[64,2048]{1,0:T(8,128)(2,1)S(1)} %copy-done.8), channel_id=1, source_target_pairs={{0,3},{1,0},{2,1},{3,2},{4,7},{5,4},{6,5},{7,6},{8,11},{9,8},{10,9... | collective-permute-start | bytes 786440 | tf_op jit(solution)/shard_map/ppermute | solution.py:422
  42.6 1.8 %intra.1 = (f32[256,512]{1,0:T(8,128)S(1)}, bf16[256,1024]{1,0:T(8,128)(2,1)S(1)}) custom-call(bf16[64,256]{1,0:T(8,128)(2,1)} %bitcast.18, bf16[64,256]{1,0:T(8,128)(2,1)} %bitcast.15, bf16[256,512]{1,0:T(8,128)(2,1)S(1)} %get-tuple-element.69.value, f32[256,4]{1,0:T(8,128)S(1)} %get-tuple-element.75.cum, f32[4,1,256]{2,1,0:T(1,128)S(1)} %get-tuple-element.76.cum_row, ...), custom_call_target="tpu_custom_call" | custom-call | tf_op jit(solution)/shard_map/intra/pallas_call | solution.py:470
  44.4 2.2 %window.1 = (bf16[256,512]{1,0:T(8,128)(2,1)S(1)}, bf16[256,512]{1,0:T(8,128)(2,1)S(1)}) custom-call(s32[4]{0:T(128)S(1)} %copy-done.7, s32[1]{0:T(128)} %bitcast.3.first_col, bf16[256,512]{1,0:T(8,128)(2,1)S(1)} %get-tuple-element.67.query, bf16[256,512]{1,0:T(8,128)(2,1)S(1)} %get-tuple-element.68.key, bf16[256,512]{1,0:T(8,128)(2,1)S(1)} %get-tuple-element.69.value, ...), custom_call_target="tpu_custom_call" | custom-call | tf_op jit(solution)/shard_map/window/pallas_call | solution.py:478
  46.6 2.0 %collective-permute-done.2.piece1 = bf16[64,2048]{1,0:T(8,128)(2,1)} collective-permute-done((bf16[64,2048]{1,0:T(8,128)(2,1)S(1)}, bf16[64,2048]{1,0:T(8,128)(2,1)}, u32[]{:S(2)}, u32[]{:S(2)}) %collective-permute-start.2) | collective-permute-done | bytes 262176 | tf_op jit(solution)/shard_map/ppermute | solution.py:422
  48.6 2.7 %grad_mixed.1.grad = bf16[256,512]{1,0:T(8,128)(2,1)S(1)} custom-call(s32[1]{0:T(128)} %bitcast.4.place, bf16[64,2048]{1,0:T(8,128)(2,1)} %piece0.1, bf16[64,2048]{1,0:T(8,128)(2,1)} %collective-permute-done.2.piece1, bf16[64,2048]{1,0:T(8,128)(2,1)} %copy-done.9, bf16[64,2048]{1,0:T(8,128)(2,1)} %collective-permute-done.3.piece3, bf16[512,2048]{1,0:T(8,128)(2,1)} %weight_far.3), custom_call_target="tpu_custom_call" | custom-call | tf_op jit(solution)/shard_map/grad_mixed/pallas_call | solution.py:484
  51.8 2.3 %mix.1 = (bf16[1024,128]{1,0:T(8,128)(2,1)}, bf16[256,512]{1,0:T(8,128)(2,1)S(1)}, bf16[256,512]{1,0:T(8,128)(2,1)S(1)}) custom-call(bf16[1024,128]{1,0:T(8,128)(2,1)S(1)} %bitcast.11, bf16[256,1024]{1,0:T(8,128)(2,1)S(1)} %get-tuple-element.80.phi, bf16[64,256]{1,0:T(8,128)(2,1)S(1)} %bitcast.20, bf16[512,16]{1,0:T(8,128)(2,1)S(1)} %copy-done, ...), custom_call_target="tpu_custom_call" | custom-call | tf_op jit(solution)/shard_map/mix/pallas_call | solution.py:502
  54.1 10.8 %all-to-all-start.2 = ((bf16[64,16,128]{2,1,0:T(8,128)(2,1)}), bf16[64,16,128]{2,1,0:T(8,128)(2,1)S(1)}, u32[]{:S(2)}, u32[]{:S(2)}) async-start(bf16[64,16,128]{2,1,0:T(8,128)(2,1)} %bitcast.22), calls=%async_computation.2 | async-start | bytes 524288 | tf_op jit(solution)/shard_map/all_to_all | solution.py:404
  64.9 3.2 %project.1 = (bf16[64,2048]{1,0:T(8,128)(2,1)}, bf16[64,2048]{1,0:T(8,128)(2,1)}, bf16[64,2048]{1,0:T(8,128)(2,1)}, bf16[64,2048]{1,0:T(8,128)(2,1)}) custom-call(s32[1]{0:T(128)} %bitcast.4.place, bf16[256,512]{1,0:T(8,128)(2,1)S(1)} %get-tuple-element.87.mixed, bf16[512,2048]{1,0:T(8,128)(2,1)} %weight_far.3), custom_call_target="tpu_custom_call" | custom-call | tf_op jit(solution)/shard_map/project/pallas_call | solution.py:512
  68.8 3.3 %collective-permute-start.5 = (bf16[64,2048]{1,0:T(8,128)(2,1)}, bf16[64,2048]{1,0:T(8,128)(2,1)}, u32[]{:S(2)}, u32[]{:S(2)}) collective-permute-start(bf16[64,2048]{1,0:T(8,128)(2,1)} %get-tuple-element.98), channel_id=1, source_target_pairs={{0,2},{1,3},{2,0},{3,1},{4,6},{5,7},{6,4},{7,5},{8,10},{9,11},{10,... | collective-permute-start | bytes 786440 | tf_op jit(solution)/shard_map/ppermute | solution.py:422
  72.1 4.8 %all-to-all-done.2.a = bf16[64,16,128]{2,1,0:T(8,128)(2,1)S(1)} async-done(((bf16[64,16,128]{2,1,0:T(8,128)(2,1)}), bf16[64,16,128]{2,1,0:T(8,128)(2,1)S(1)}, u32[]{:S(2)}, u32[]{:S(2)}) %all-to-all-start.2) | async-done | bytes 262176 | tf_op jit(solution)/shard_map/all_to_all | solution.py:404
  77.8 6.3 %all-to-all-start.3 = ((bf16[64,16,128]{2,1,0:T(8,128)(2,1)}), bf16[64,16,128]{2,1,0:T(8,128)(2,1)S(1)}, u32[]{:S(2)}, u32[]{:S(2)}) async-start(bf16[64,16,128]{2,1,0:T(8,128)(2,1)} %chain_back.1), calls=%async_computation.3 | async-start | bytes 524288 | tf_op jit(solution)/shard_map/all_to_all | solution.py:404
  84.1 3.9 %intra_grad.1 = (bf16[64,256]{1,0:T(8,128)(2,1)}, f32[64,256]{1,0:T(8,128)S(1)}, f32[256,512]{1,0:T(8,128)S(1)}, bf16[256,1024]{1,0:T(8,128)(2,1)S(1)}) custom-call(bf16[64,256]{1,0:T(8,128)(2,1)} %bitcast.19, bf16[64,256]{1,0:T(8,128)(2,1)} %bitcast.16, bf16[256,512]{1,0:T(8,128)(2,1)} %value.5, f32[256,4]{1,0:T(8,128)S(1)} %get-tuple-element.75.cum, ...), custom_call_target="tpu_custom_call" | custom-call | tf_op jit(solution)/shard_map/intra_grad/pallas_call | solution.py:545
  88.1 2.3 %edge_grad.1 = bf16[128,512]{1,0:T(8,128)(2,1)} custom-call(bf16[256,512]{1,0:T(8,128)(2,1)} %query.3, bf16[256,512]{1,0:T(8,128)(2,1)} %value.5, bf16[128,512]{1,0:T(8,128)(2,1)S(1)} %collective-permute-done.before, bf16[256,512]{1,0:T(8,128)(2,1)S(1)} %get-tuple-element.101.probs, bf16[256,512]{1,0:T(8,128)(2,1)S(1)} %grad_mixed.1.grad), custom_call_target="tpu_custom_call" | custom-call | tf_op jit(solution)/shard_map/edge_grad/pallas_call | solution.py:530
  90.4 2.4 %collective-permute-start.7 = (bf16[128,512]{1,0:T(8,128)(2,1)}, bf16[128,512]{1,0:T(8,128)(2,1)S(1)}, u32[]{:S(2)}, u32[]{:S(2)}) collective-permute-start(bf16[128,512]{1,0:T(8,128)(2,1)} %edge_grad.1), channel_id=1, source_target_pairs={{4,0},{8,4},{12,8},{16,12},{20,16},{24,20},{28,24},{32,28},{36,32}... | collective-permute-start | bytes 393224 | tf_op jit(solution)/shard_map/ppermute | solution.py:536
  92.8 1.9 %add_convert_fusion = bf16[64,2048]{1,0:T(8,128)(2,1)} fusion(bf16[64,2048]{1,0:T(8,128)(2,1)} %collective-permute-done.6, bf16[64,2048]{1,0:T(8,128)(2,1)} %collective-permute-done.5, bf16[64,2048]{1,0:T(8,128)(2,1)S(1)} %collective-permute-done.4, bf16[64,2048]{1,0:T(8,128)(2,1)S(1)} %copy-done.10), kind=kLoop, calls=%fused_computation | loop fusion | flops 1048576 | bytes 1310720 | tf_op jit(solution)/shard_map/convert_element_type | solution.py:559
  94.7 3.6 %window_grad.1 = (bf16[256,512]{1,0:T(8,128)(2,1)}, bf16[256,512]{1,0:T(8,128)(2,1)S(1)}, bf16[256,512]{1,0:T(8,128)(2,1)S(1)}) custom-call(bf16[256,512]{1,0:T(8,128)(2,1)} %query.3, bf16[256,512]{1,0:T(8,128)(2,1)} %key.1, bf16[256,512]{1,0:T(8,128)(2,1)} %value.5, bf16[128,512]{1,0:T(8,128)(2,1)S(1)} %collective-permute-done.before, ...), custom_call_target="tpu_custom_call" | custom-call | tf_op jit(solution)/shard_map/window_grad/pallas_call | solution.py:538
  98.3 2.3 %finish.1 = (bf16[256,512]{1,0:T(8,128)(2,1)}, bf16[256,512]{1,0:T(8,128)(2,1)}, bf16[64,256]{1,0:T(8,128)(2,1)}) custom-call(bf16[64,256]{1,0:T(8,128)(2,1)S(1)} %bitcast.17, bf16[256,1024]{1,0:T(8,128)(2,1)S(1)} %get-tuple-element.106.phi, bf16[256,512]{1,0:T(8,128)(2,1)S(1)} %copy-done.4, f32[256,4]{1,0:T(8,128)S(1)} %get-tuple-element.75.cum, ...), custom_call_target="tpu_custom_call" | custom-call | tf_op jit(solution)/shard_map/finish/pallas_call | solution.py:565
  (35 shorter events, 3.5 us)
Async XLA Ops:
  0.6 39.2 %copy-start.8 = (bf16[64,2048]{1,0:T(8,128)(2,1)S(1)}, bf16[64,2048]{1,0:T(8,128)(2,1)}, u32[]{:S(2)}) copy-start(bf16[64,2048]{1,0:T(8,128)(2,1)} %piece0.1) | copy-start | bytes 786436
  0.6 43.7 %copy-start.7 = (s32[4]{0:T(128)S(1)}, s32[4]{0:T(128)}, u32[]{:S(2)}) copy-start(s32[4]{0:T(128)} %band.1) | copy-start | bytes 52
  4.6 25.2 %all-to-all-start = ((bf16[64,16,128]{2,1,0:T(8,128)(2,1)}), bf16[64,16,128]{2,1,0:T(8,128)(2,1)S(1)}, u32[]{:S(2)}, u32[]{:S(2)}) async-start(bf16[64,16,128]{2,1,0:T(8,128)(2,1)} %bitcast.23), calls=%async_computation | async-start | bytes 524288 | tf_op jit(solution)/shard_map/all_to_all | solution.py:404
  17.8 9.2 %collective-permute-start.1 = (bf16[64,2048]{1,0:T(8,128)(2,1)}, bf16[64,2048]{1,0:T(8,128)(2,1)S(1)}, u32[]{:S(2)}, u32[]{:S(2)}) collective-permute-start(bf16[64,2048]{1,0:T(8,128)(2,1)} %piece0.1), channel_id=1, source_target_pairs={{0,2},{1,3},{2,0},{3,1},{4,6},{5,7},{6,4},{7,5},{8,10},{9,11},{10,... | collective-permute-start | bytes 786440 | tf_op jit(solution)/shard_map/ppermute | solution.py:422
  20.6 6.4 %collective-permute-start = (bf16[128,512]{1,0:T(8,128)(2,1)}, bf16[128,512]{1,0:T(8,128)(2,1)S(1)}, u32[]{:S(2)}, u32[]{:S(2)}) collective-permute-start(bf16[128,512]{1,0:T(8,128)(2,1)} %get-tuple-element.63), channel_id=1, source_target_pairs={{0,4},{4,8},{8,12},{12,16},{16,20},{20,24},{24,28},{28,32},{32,36}... | collective-permute-start | bytes 393224 | tf_op jit(solution)/shard_map/ppermute | solution.py:461
  27.0 15.5 %copy-start.9 = (bf16[64,2048]{1,0:T(8,128)(2,1)}, bf16[64,2048]{1,0:T(8,128)(2,1)S(1)}, u32[]{:S(2)}) copy-start(bf16[64,2048]{1,0:T(8,128)(2,1)S(1)} %collective-permute-done.1.piece2) | copy-start | bytes 786436
  30.7 21.1 %all-to-all-start.1 = ((bf16[64,16,128]{2,1,0:T(8,128)(2,1)}), bf16[64,16,128]{2,1,0:T(8,128)(2,1)S(1)}, u32[]{:S(2)}, u32[]{:S(2)}) async-start(bf16[64,16,128]{2,1,0:T(8,128)(2,1)} %chain_fwd.1), calls=%async_computation.1 | async-start | bytes 524288 | tf_op jit(solution)/shard_map/all_to_all | solution.py:404
  39.8 8.8 %collective-permute-start.2 = (bf16[64,2048]{1,0:T(8,128)(2,1)S(1)}, bf16[64,2048]{1,0:T(8,128)(2,1)}, u32[]{:S(2)}, u32[]{:S(2)}) collective-permute-start(bf16[64,2048]{1,0:T(8,128)(2,1)S(1)} %copy-done.8), channel_id=1, source_target_pairs={{0,1},{1,2},{2,3},{3,0},{4,5},{5,6},{6,7},{7,4},{8,9},{9,10},{10,1... | collective-permute-start | bytes 786440 | tf_op jit(solution)/shard_map/ppermute | solution.py:422
  40.4 8.2 %collective-permute-start.3 = (bf16[64,2048]{1,0:T(8,128)(2,1)S(1)}, bf16[64,2048]{1,0:T(8,128)(2,1)}, u32[]{:S(2)}, u32[]{:S(2)}) collective-permute-start(bf16[64,2048]{1,0:T(8,128)(2,1)S(1)} %copy-done.8), channel_id=1, source_target_pairs={{0,3},{1,0},{2,1},{3,2},{4,7},{5,4},{6,5},{7,6},{8,11},{9,8},{10,9... | collective-permute-start | bytes 786440 | tf_op jit(solution)/shard_map/ppermute | solution.py:422
  44.4 7.4 %copy-start = (bf16[512,16]{1,0:T(8,128)(2,1)S(1)}, bf16[512,16]{1,0:T(8,128)(2,1)}, u32[]{:S(2)}) copy-start(bf16[512,16]{1,0:T(8,128)(2,1)} %constant.23.clone.sel) | copy-start | bytes 49156
  44.4 7.4 %copy-start.3 = (bf16[256,64]{0,1:T(8,128)(2,1)S(1)}, bf16[256,64]{0,1:T(8,128)(2,1)}, u32[]{:S(2)}) copy-start(bf16[256,64]{0,1:T(8,128)(2,1)} %param.17) | copy-start | bytes 98308
  44.4 7.4 %copy-start.6 = (f32[512]{0:T(512)S(1)}, f32[512]{0:T(512)}, u32[]{:S(2)}) copy-start(f32[512]{0:T(512)} %param.21) | copy-start | bytes 6148
  54.1 22.8 %all-to-all-start.2 = ((bf16[64,16,128]{2,1,0:T(8,128)(2,1)}), bf16[64,16,128]{2,1,0:T(8,128)(2,1)S(1)}, u32[]{:S(2)}, u32[]{:S(2)}) async-start(bf16[64,16,128]{2,1,0:T(8,128)(2,1)} %bitcast.22), calls=%async_computation.2 | async-start | bytes 524288 | tf_op jit(solution)/shard_map/all_to_all | solution.py:404
  68.1 24.6 %copy-start.10 = (bf16[64,2048]{1,0:T(8,128)(2,1)S(1)}, bf16[64,2048]{1,0:T(8,128)(2,1)}, u32[]{:S(2)}) copy-start(bf16[64,2048]{1,0:T(8,128)(2,1)} %get-tuple-element.96) | copy-start | bytes 786436
  68.2 24.6 %collective-permute-start.4 = (bf16[64,2048]{1,0:T(8,128)(2,1)}, bf16[64,2048]{1,0:T(8,128)(2,1)S(1)}, u32[]{:S(2)}, u32[]{:S(2)}) collective-permute-start(bf16[64,2048]{1,0:T(8,128)(2,1)} %get-tuple-element.97), channel_id=1, source_target_pairs={{0,1},{1,2},{2,3},{3,0},{4,5},{5,6},{6,7},{7,4},{8,9},{9,10},{10,1... | collective-permute-start | bytes 786440 | tf_op jit(solution)/shard_map/ppermute | solution.py:422
  68.8 23.9 %collective-permute-start.5 = (bf16[64,2048]{1,0:T(8,128)(2,1)}, bf16[64,2048]{1,0:T(8,128)(2,1)}, u32[]{:S(2)}, u32[]{:S(2)}) collective-permute-start(bf16[64,2048]{1,0:T(8,128)(2,1)} %get-tuple-element.98), channel_id=1, source_target_pairs={{0,2},{1,3},{2,0},{3,1},{4,6},{5,7},{6,4},{7,5},{8,10},{9,11},{10,... | collective-permute-start | bytes 786440 | tf_op jit(solution)/shard_map/ppermute | solution.py:422
  72.1 20.6 %collective-permute-start.6 = (bf16[64,2048]{1,0:T(8,128)(2,1)}, bf16[64,2048]{1,0:T(8,128)(2,1)}, u32[]{:S(2)}, u32[]{:S(2)}) collective-permute-start(bf16[64,2048]{1,0:T(8,128)(2,1)} %get-tuple-element.99), channel_id=1, source_target_pairs={{0,3},{1,0},{2,1},{3,2},{4,7},{5,4},{6,5},{7,6},{8,11},{9,8},{10,9... | collective-permute-start | bytes 786440 | tf_op jit(solution)/shard_map/ppermute | solution.py:422
  77.8 20.5 %all-to-all-start.3 = ((bf16[64,16,128]{2,1,0:T(8,128)(2,1)}), bf16[64,16,128]{2,1,0:T(8,128)(2,1)S(1)}, u32[]{:S(2)}, u32[]{:S(2)}) async-start(bf16[64,16,128]{2,1,0:T(8,128)(2,1)} %chain_back.1), calls=%async_computation.3 | async-start | bytes 524288 | tf_op jit(solution)/shard_map/all_to_all | solution.py:404
  88.1 10.2 %copy-start.1 = (bf16[512,16]{1,0:T(8,128)(2,1)S(1)}, bf16[512,16]{1,0:T(8,128)(2,1)}, u32[]{:S(2)}) copy-start(bf16[512,16]{1,0:T(8,128)(2,1)} %constant.21.clone.sel) | copy-start | bytes 49156
  88.1 10.2 %copy-start.2 = (bf16[256,64]{0,1:T(8,128)(2,1)S(1)}, bf16[256,64]{0,1:T(8,128)(2,1)}, u32[]{:S(2)}) copy-start(bf16[256,64]{0,1:T(8,128)(2,1)} %param.18) | copy-start | bytes 98308
  88.1 10.2 %copy-start.4 = (bf16[256,512]{1,0:T(8,128)(2,1)S(1)}, bf16[256,512]{1,0:T(8,128)(2,1)}, u32[]{:S(2)}) copy-start(bf16[256,512]{1,0:T(8,128)(2,1)} %get-tuple-element.107.faded) | copy-start | bytes 786436
  88.1 10.2 %copy-start.5 = (bf16[16,512]{1,0:T(8,128)(2,1)S(1)}, bf16[16,512]{1,0:T(8,128)(2,1)}, u32[]{:S(2)}) copy-start(bf16[16,512]{1,0:T(8,128)(2,1)} %constant.22.clone.sel_kt.sel_t) | copy-start | bytes 49156
  90.4 7.9 %collective-permute-start.7 = (bf16[128,512]{1,0:T(8,128)(2,1)}, bf16[128,512]{1,0:T(8,128)(2,1)S(1)}, u32[]{:S(2)}, u32[]{:S(2)}) collective-permute-start(bf16[128,512]{1,0:T(8,128)(2,1)} %edge_grad.1), channel_id=1, source_target_pairs={{4,0},{8,4},{12,8},{16,12},{20,16},{24,20},{28,24},{32,28},{36,32}... | collective-permute-start | bytes 393224 | tf_op jit(solution)/shard_map/ppermute | solution.py:536

commit v3 on v2

--- a/solution.py
+++ b/solution.py
@@ -176,27 +176,38 @@
     return jnp.concatenate(parts, axis=0)
 
 
-def grad_mixed_kernel(
-    place, piece0, piece1, piece2, piece3, weight_far, grad_out, rows, weight, sems
-):
-    pieces = (piece0, piece1, piece2, piece3)
-    half = weight.shape[0] // 2
-    copies = []
-    for k, piece in enumerate(pieces):
-        at = ((place[0] + (len(pieces) - k)) % len(pieces)) * WINDOW
-        to = rows.at[pl.ds(pl.multiple_of(at, WINDOW), WINDOW), :]
-        copies.append(pltpu.make_async_copy(piece, to, sems.at[k]))
-    copies.append(pltpu.make_async_copy(weight_far, weight, sems.at[4]))
+def rows_of(lane, ways, k):
+    return pl.ds(pl.multiple_of(((lane + (ways - k)) % ways) * WINDOW, WINDOW), WINDOW)
+
+
+def grad_mixed_kernel(place, piece1, piece3, weight, early, grad_out, rows, sems):
+    ways = grad_out.shape[0] // WINDOW
+    copies = [
+        pltpu.make_async_copy(piece, rows.at[i * WINDOW : (i + 1) * WINDOW, :], sems.at[i])
+        for i, piece in enumerate((piece1, piece3))
+    ]
     for copy in copies:
         copy.start()
+    for i, k in enumerate((0, 2)):
+        grad_out[rows_of(place[0], ways, k), :] = early[i * WINDOW : (i + 1) * WINDOW, :]
     for copy in copies:
         copy.wait()
-    for i in range(2):
-        part = slice(i * half, (i + 1) * half)
-        grad_out[:, part] = mm(rows[...], weight[part, :], NT).astype(BF16)
-
-
-def window_kernel(band, first_col, query, key, value, before, attended_out, probs_out):
+    grad = mm(rows[...], weight[...], NT).astype(BF16)
+    for i, k in enumerate((1, 3)):
+        grad_out[rows_of(place[0], ways, k), :] = grad[i * WINDOW : (i + 1) * WINDOW, :]
+
+
+def window_kernel(
+    band, first_col, query, key, value, before, own, piece2, weight_far,
+    attended_out, probs_out, grad_out, weight, rows, sems
+):
+    copies = [
+        pltpu.make_async_copy(own, rows.at[:WINDOW, :], sems.at[0]),
+        pltpu.make_async_copy(piece2, rows.at[WINDOW:, :], sems.at[1]),
+        pltpu.make_async_copy(weight_far, weight, sems.at[2]),
+    ]
+    for copy in copies:
+        copy.start()
     row = lax.broadcasted_iota(jnp.int32, (WINDOW, 2 * WINDOW), 0)
     col = lax.broadcasted_iota(jnp.int32, (WINDOW, 2 * WINDOW), 1)
     back = WINDOW + row - col
@@ -219,6 +230,9 @@
             values = block_pair(before[WINDOW:, cols], value.at[:, cols], b)
             probs_out[here, cols] = mine
             attended_out[here, cols] = mm(mine, values, NN).astype(BF16)
+    for copy in copies:
+        copy.wait()
+    grad_out[...] = mm(rows[...], weight[...], NT).astype(BF16)
 
 
 def score_grads(probs32, grad_probs):
@@ -475,24 +489,26 @@
     )(*far(fq_late), fk_t, *near(value, cum, cum_row), sel_qt)
 
     first_col = jnp.where(place == 0, WINDOW, 0).astype(jnp.int32)[None]
-    attended, probs = kernel(
+    attended, probs, grad_early, weight = kernel(
         window_kernel,
         "window",
-        [SCALARS] * 2 + [NEAR] * 4,
-        [VMEM((count, width), BF16)] * 2,
-    )(band_width, first_col, *near(query, key, value, before))
+        [SCALARS] * 2 + [NEAR] * 4 + [FAR] * 3,
+        [VMEM((count, width), BF16)] * 2
+        + [VMEM((2 * WINDOW, width), BF16), VMEM(out_weight.shape, BF16)],
+        8,
+        [pltpu.VMEM((2 * WINDOW, model), BF16), pltpu.SemaphoreType.DMA((3,))],
+    )(
+        band_width, first_col, *near(query, key, value, before),
+        *far(grad_out, pieces[2], out_weight),
+    )
     grad = kernel(
         grad_mixed_kernel,
         "grad_mixed",
-        [SCALARS] + [FAR] * 5,
+        [SCALARS] + [FAR] * 2 + [NEAR] * 2,
         [VMEM((count, width), BF16)],
-        12,
-        [
-            pltpu.VMEM((count, model), BF16),
-            pltpu.VMEM(out_weight.shape, BF16),
-            pltpu.SemaphoreType.DMA((5,)),
-        ],
-    )(lane, *far(*pieces, out_weight))[0]
+        8,
+        [pltpu.VMEM((2 * WINDOW, model), BF16), pltpu.SemaphoreType.DMA((2,))],
+    )(lane, *far(pieces[1], pieces[3]), *near(weight, grad_early))[0]
 
     prefix, attended, probs, grad, local, phi = after(
         prefix, attended, probs, grad, local, phi

time: 103 us -> 102 us (level)
  the two profiles are of different devices: /device:TPU:1 before, /device:TPU:26 now
where the time goes in v3:
time: 102 us
  starting transfers between devices  55.3 us (54%)
  Pallas kernels  31.1 us (30%)
  waiting for transfers between devices  11.8 us (12%)
  other arithmetic  1.87 us (2%)
    all_to_all x4, starting transfers between devices, swap(): return lax.all_to_all(value, 'seq', split_axis=0, concat_axis=0, tiled=True)  38.8 us
    ppermute x6, starting transfers between devices, shifted(): return lax.ppermute(value, 'mp', [(i, (i + k) % ways) for i in range(ways)])  9.99 us
    ppermute x1, waiting for transfers between devices, body(): before = lax.ppermute(edge, 'seq', [(i, i + 1) for i in range(peers - 1)])  7.03 us
    ppermute x1, starting transfers between devices, body(): lax.ppermute(edge_grad, 'seq', [(i + 1, i) for i in range(peers - 1)])  4.6 us
    pallas_call x1, Pallas kernels, body(): kernel(window_kernel, 'window', [SCALARS] * 2 + [NEAR] * 4 + [FAR] * 3, [...  4.36 us
    pallas_call x1, Pallas kernels, body(): kernel(intra_grad_kernel, 'intra_grad', [NEAR] * 10, [HBM((HEADS * FEAT,...  3.94 us
    pallas_call x1, Pallas kernels, body(): kernel(local_state_kernel, 'local_state', [NEAR] * 3 + [FAR] * 3, [HBM(st...  3.93 us
    pallas_call x1, Pallas kernels, body(): kernel(window_grad_kernel, 'window_grad', [NEAR] * 6, [HBM((count, width)...  3.54 us
  transfers between devices with their start and end apart: 12, of which 5 were waited for; matrix products, arithmetic and copies ran while one was open for 2% of the time, Pallas kernels for 21%

profile of v3, /device:TPU:26, one launch (start us, length us, event | category | flops | bytes accessed | tf_op | source)
XLA Modules:
  0.0 101.8 jit_solution(7621749326121275757)
XLA Ops:
  0.6 3.9 %local_state.1 = (bf16[1024,128]{1,0:T(8,128)(2,1)}, f32[256,4]{1,0:T(8,128)S(1)}, f32[4,1,256]{2,1,0:T(1,128)S(1)}, bf16[128,512]{1,0:T(8,128)(2,1)}, bf16[256,...) custom-call(bf16[64,256]{1,0:T(8,128)(2,1)} %bitcast.14, ...), custom_call_target="tpu_custom_call" | custom-call | tf_op jit(solution)/shard_map/local_state/pallas_call | solution.py:455
  4.6 12.1 %all-to-all-start = ((bf16[64,16,128]{2,1,0:T(8,128)(2,1)}), bf16[64,16,128]{2,1,0:T(8,128)(2,1)S(1)}, u32[]{:S(2)}, u32[]{:S(2)}) async-start(bf16[64,16,128]{2,1,0:T(8,128)(2,1)} %bitcast.23), calls=%async_computation | async-start | bytes 524288 | tf_op jit(solution)/shard_map/all_to_all | solution.py:418
  16.7 2.2 %collective-permute-start.1 = (bf16[64,2048]{1,0:T(8,128)(2,1)}, bf16[64,2048]{1,0:T(8,128)(2,1)S(1)}, u32[]{:S(2)}, u32[]{:S(2)}) collective-permute-start(bf16[64,2048]{1,0:T(8,128)(2,1)} %own.1), channel_id=1, source_target_pairs={{0,2},{1,3},{2,0},{3,1},{4,6},{5,7},{6,4},{7,5},{8,10},{9,11},{10,... | collective-permute-start | bytes 786440 | tf_op jit(solution)/shard_map/ppermute | solution.py:436
  18.9 1.9 %collective-permute-start = (bf16[128,512]{1,0:T(8,128)(2,1)}, bf16[128,512]{1,0:T(8,128)(2,1)S(1)}, u32[]{:S(2)}, u32[]{:S(2)}) collective-permute-start(bf16[128,512]{1,0:T(8,128)(2,1)} %get-tuple-element.65), channel_id=1, source_target_pairs={{0,4},{4,8},{8,12},{12,16},{16,20},{20,24},{24,28},{28,32},{32,36}... | collective-permute-start | bytes 393224 | tf_op jit(solution)/shard_map/ppermute | solution.py:475
  20.8 7.0 %collective-permute-done.before = bf16[128,512]{1,0:T(8,128)(2,1)S(1)} collective-permute-done((bf16[128,512]{1,0:T(8,128)(2,1)}, bf16[128,512]{1,0:T(8,128)(2,1)S(1)}, u32[]{:S(2)}, u32[]{:S(2)}) %collective-permute-start) | collective-permute-done | bytes 131104 | tf_op jit(solution)/shard_map/ppermute | solution.py:475
  29.3 8.7 %all-to-all-start.1 = ((bf16[64,16,128]{2,1,0:T(8,128)(2,1)}), bf16[64,16,128]{2,1,0:T(8,128)(2,1)S(1)}, u32[]{:S(2)}, u32[]{:S(2)}) async-start(bf16[64,16,128]{2,1,0:T(8,128)(2,1)} %chain_fwd.1), calls=%async_computation.1 | async-start | bytes 524288 | tf_op jit(solution)/shard_map/all_to_all | solution.py:418
  38.0 1.6 %collective-permute-start.2 = (bf16[64,2048]{1,0:T(8,128)(2,1)}, bf16[64,2048]{1,0:T(8,128)(2,1)S(1)}, u32[]{:S(2)}, u32[]{:S(2)}) collective-permute-start(bf16[64,2048]{1,0:T(8,128)(2,1)} %own.1), channel_id=1, source_target_pairs={{0,1},{1,2},{2,3},{3,0},{4,5},{5,6},{6,7},{7,4},{8,9},{9,10},{10,1... | collective-permute-start | bytes 786440 | tf_op jit(solution)/shard_map/ppermute | solution.py:436
  40.1 1.8 %intra.1 = (f32[256,512]{1,0:T(8,128)S(1)}, bf16[256,1024]{1,0:T(8,128)(2,1)S(1)}) custom-call(bf16[64,256]{1,0:T(8,128)(2,1)} %bitcast.18, bf16[64,256]{1,0:T(8,128)(2,1)} %bitcast.15, bf16[256,512]{1,0:T(8,128)(2,1)S(1)} %get-tuple-element.71.value, f32[256,4]{1,0:T(8,128)S(1)} %get-tuple-element.79.cum, f32[4,1,256]{2,1,0:T(1,128)S(1)} %get-tuple-element.80.cum_row, ...), custom_call_target="tpu_custom_call" | custom-call | tf_op jit(solution)/shard_map/intra/pallas_call | solution.py:484
  41.9 4.4 %window.1 = (bf16[256,512]{1,0:T(8,128)(2,1)S(1)}, bf16[256,512]{1,0:T(8,128)(2,1)S(1)}, bf16[128,512]{1,0:T(8,128)(2,1)S(1)}, bf16[512,2048]{1,0:T(8,128)(2,1)S(1)}) custom-call(s32[4]{0:T(128)S(1)} %copy-done.7, s32[1]{0:T(128)} %bitcast.3.first_col, bf16[256,512]{1,0:T(8,128)(2,1)S(1)} %get-tuple-element.69.query, ...), custom_call_target="tpu_custom_call" | custom-call | tf_op jit(solution)/shard_map/window/pallas_call | solution.py:492
  48.6 1.9 %grad_mixed.1.grad = bf16[256,512]{1,0:T(8,128)(2,1)S(1)} custom-call(s32[1]{0:T(128)} %bitcast.4.place, bf16[64,2048]{1,0:T(8,128)(2,1)} %copy-done.9, bf16[64,2048]{1,0:T(8,128)(2,1)} %copy-done.10, bf16[512,2048]{1,0:T(8,128)(2,1)S(1)} %get-tuple-element.76.weight, bf16[128,512]{1,0:T(8,128)(2,1)S(1)} %get-tuple-element.77.early), custom_call_target="tpu_custom_call" | custom-call | tf_op jit(solution)/shard_map/grad_mixed/pallas_call | solution.py:504
  50.5 2.3 %mix.1 = (bf16[1024,128]{1,0:T(8,128)(2,1)}, bf16[256,512]{1,0:T(8,128)(2,1)S(1)}, bf16[256,512]{1,0:T(8,128)(2,1)S(1)}) custom-call(bf16[1024,128]{1,0:T(8,128)(2,1)S(1)} %bitcast.11, bf16[256,1024]{1,0:T(8,128)(2,1)S(1)} %get-tuple-element.84.phi, bf16[64,256]{1,0:T(8,128)(2,1)S(1)} %bitcast.20, bf16[512,16]{1,0:T(8,128)(2,1)S(1)} %copy-done, ...), custom_call_target="tpu_custom_call" | custom-call | tf_op jit(solution)/shard_map/mix/pallas_call | solution.py:518
  52.8 10.3 %all-to-all-start.2 = ((bf16[64,16,128]{2,1,0:T(8,128)(2,1)}), bf16[64,16,128]{2,1,0:T(8,128)(2,1)S(1)}, u32[]{:S(2)}, u32[]{:S(2)}) async-start(bf16[64,16,128]{2,1,0:T(8,128)(2,1)} %bitcast.22), calls=%async_computation.2 | async-start | bytes 524288 | tf_op jit(solution)/shard_map/all_to_all | solution.py:418
  63.1 3.2 %project.1 = (bf16[64,2048]{1,0:T(8,128)(2,1)}, bf16[64,2048]{1,0:T(8,128)(2,1)}, bf16[64,2048]{1,0:T(8,128)(2,1)}, bf16[64,2048]{1,0:T(8,128)(2,1)}) custom-call(s32[1]{0:T(128)} %bitcast.4.place, bf16[256,512]{1,0:T(8,128)(2,1)S(1)} %get-tuple-element.91.mixed, bf16[512,2048]{1,0:T(8,128)(2,1)} %weight_far.3), custom_call_target="tpu_custom_call" | custom-call | tf_op jit(solution)/shard_map/project/pallas_call | solution.py:528
  66.3 1.3 %collective-permute-start.4 = (bf16[64,2048]{1,0:T(8,128)(2,1)}, bf16[64,2048]{1,0:T(8,128)(2,1)S(1)}, u32[]{:S(2)}, u32[]{:S(2)}) collective-permute-start(bf16[64,2048]{1,0:T(8,128)(2,1)} %get-tuple-element.101), channel_id=1, source_target_pairs={{0,1},{1,2},{2,3},{3,0},{4,5},{5,6},{6,7},{7,4},{8,9},{9,10},{10,1... | collective-permute-start | bytes 786440 | tf_op jit(solution)/shard_map/ppermute | solution.py:436
  67.6 2.1 %collective-permute-start.5 = (bf16[64,2048]{1,0:T(8,128)(2,1)}, bf16[64,2048]{1,0:T(8,128)(2,1)}, u32[]{:S(2)}, u32[]{:S(2)}) collective-permute-start(bf16[64,2048]{1,0:T(8,128)(2,1)} %get-tuple-element.102), channel_id=1, source_target_pairs={{0,2},{1,3},{2,0},{3,1},{4,6},{5,7},{6,4},{7,5},{8,10},{9,11},{10,... | collective-permute-start | bytes 786440 | tf_op jit(solution)/shard_map/ppermute | solution.py:436
  69.8 2.3 %collective-permute-start.6 = (bf16[64,2048]{1,0:T(8,128)(2,1)}, bf16[64,2048]{1,0:T(8,128)(2,1)}, u32[]{:S(2)}, u32[]{:S(2)}) collective-permute-start(bf16[64,2048]{1,0:T(8,128)(2,1)} %get-tuple-element.103), channel_id=1, source_target_pairs={{0,3},{1,0},{2,1},{3,2},{4,7},{5,4},{6,5},{7,6},{8,11},{9,8},{10,9... | collective-permute-start | bytes 786440 | tf_op jit(solution)/shard_map/ppermute | solution.py:436
  72.0 2.6 %all-to-all-done.2.a = bf16[64,16,128]{2,1,0:T(8,128)(2,1)S(1)} async-done(((bf16[64,16,128]{2,1,0:T(8,128)(2,1)}), bf16[64,16,128]{2,1,0:T(8,128)(2,1)S(1)}, u32[]{:S(2)}, u32[]{:S(2)}) %all-to-all-start.2) | async-done | bytes 262176 | tf_op jit(solution)/shard_map/all_to_all | solution.py:418
  75.5 7.7 %all-to-all-start.3 = ((bf16[64,16,128]{2,1,0:T(8,128)(2,1)}), bf16[64,16,128]{2,1,0:T(8,128)(2,1)S(1)}, u32[]{:S(2)}, u32[]{:S(2)}) async-start(bf16[64,16,128]{2,1,0:T(8,128)(2,1)} %chain_back.1), calls=%async_computation.3 | async-start | bytes 524288 | tf_op jit(solution)/shard_map/all_to_all | solution.py:418
  83.2 3.9 %intra_grad.1 = (bf16[64,256]{1,0:T(8,128)(2,1)}, f32[64,256]{1,0:T(8,128)S(1)}, f32[256,512]{1,0:T(8,128)S(1)}, bf16[256,1024]{1,0:T(8,128)(2,1)S(1)}) custom-call(bf16[64,256]{1,0:T(8,128)(2,1)} %bitcast.19, bf16[64,256]{1,0:T(8,128)(2,1)} %bitcast.16, bf16[256,512]{1,0:T(8,128)(2,1)} %value.5, f32[256,4]{1,0:T(8,128)S(1)} %get-tuple-element.79.cum, ...), custom_call_target="tpu_custom_call" | custom-call | tf_op jit(solution)/shard_map/intra_grad/pallas_call | solution.py:561
  87.2 2.3 %edge_grad.1 = bf16[128,512]{1,0:T(8,128)(2,1)} custom-call(bf16[256,512]{1,0:T(8,128)(2,1)} %query.3, bf16[256,512]{1,0:T(8,128)(2,1)} %value.5, bf16[128,512]{1,0:T(8,128)(2,1)S(1)} %collective-permute-done.before, bf16[256,512]{1,0:T(8,128)(2,1)S(1)} %get-tuple-element.105.probs, bf16[256,512]{1,0:T(8,128)(2,1)S(1)} %grad_mixed.1.grad), custom_call_target="tpu_custom_call" | custom-call | tf_op jit(solution)/shard_map/edge_grad/pallas_call | solution.py:546
  89.4 4.6 %collective-permute-start.7 = (bf16[128,512]{1,0:T(8,128)(2,1)}, bf16[128,512]{1,0:T(8,128)(2,1)S(1)}, u32[]{:S(2)}, u32[]{:S(2)}) collective-permute-start(bf16[128,512]{1,0:T(8,128)(2,1)} %edge_grad.1), channel_id=1, source_target_pairs={{4,0},{8,4},{12,8},{16,12},{20,16},{24,20},{28,24},{32,28},{36,32}... | collective-permute-start | bytes 393224 | tf_op jit(solution)/shard_map/ppermute | solution.py:552
  94.1 1.9 %add_convert_fusion = bf16[64,2048]{1,0:T(8,128)(2,1)} fusion(bf16[64,2048]{1,0:T(8,128)(2,1)} %collective-permute-done.6, bf16[64,2048]{1,0:T(8,128)(2,1)} %collective-permute-done.5, bf16[64,2048]{1,0:T(8,128)(2,1)S(1)} %collective-permute-done.4, bf16[64,2048]{1,0:T(8,128)(2,1)S(1)} %copy-done.8), kind=kLoop, calls=%fused_computation | loop fusion | flops 1048576 | bytes 1310720 | tf_op jit(solution)/shard_map/convert_element_type | solution.py:575
  95.9 3.5 %window_grad.1 = (bf16[256,512]{1,0:T(8,128)(2,1)}, bf16[256,512]{1,0:T(8,128)(2,1)S(1)}, bf16[256,512]{1,0:T(8,128)(2,1)S(1)}) custom-call(bf16[256,512]{1,0:T(8,128)(2,1)} %query.3, bf16[256,512]{1,0:T(8,128)(2,1)} %key.1, bf16[256,512]{1,0:T(8,128)(2,1)} %value.5, bf16[128,512]{1,0:T(8,128)(2,1)S(1)} %collective-permute-done.before, ...), custom_call_target="tpu_custom_call" | custom-call | tf_op jit(solution)/shard_map/window_grad/pallas_call | solution.py:554
  99.5 2.3 %finish.1 = (bf16[256,512]{1,0:T(8,128)(2,1)}, bf16[256,512]{1,0:T(8,128)(2,1)}, bf16[64,256]{1,0:T(8,128)(2,1)}) custom-call(bf16[64,256]{1,0:T(8,128)(2,1)S(1)} %bitcast.17, bf16[256,1024]{1,0:T(8,128)(2,1)S(1)} %get-tuple-element.110.phi, bf16[256,512]{1,0:T(8,128)(2,1)S(1)} %copy-done.4, f32[256,4]{1,0:T(8,128)S(1)} %get-tuple-element.79.cum, ...), custom_call_target="tpu_custom_call" | custom-call | tf_op jit(solution)/shard_map/finish/pallas_call | solution.py:581
  (37 shorter events, 5.1 us)
Async XLA Ops:
  0.6 41.3 %copy-start.7 = (s32[4]{0:T(128)S(1)}, s32[4]{0:T(128)}, u32[]{:S(2)}) copy-start(s32[4]{0:T(128)} %band.1) | copy-start | bytes 52
  4.6 23.9 %all-to-all-start = ((bf16[64,16,128]{2,1,0:T(8,128)(2,1)}), bf16[64,16,128]{2,1,0:T(8,128)(2,1)S(1)}, u32[]{:S(2)}, u32[]{:S(2)}) async-start(bf16[64,16,128]{2,1,0:T(8,128)(2,1)} %bitcast.23), calls=%async_computation | async-start | bytes 524288 | tf_op jit(solution)/shard_map/all_to_all | solution.py:418
  16.7 11.2 %collective-permute-start.1 = (bf16[64,2048]{1,0:T(8,128)(2,1)}, bf16[64,2048]{1,0:T(8,128)(2,1)S(1)}, u32[]{:S(2)}, u32[]{:S(2)}) collective-permute-start(bf16[64,2048]{1,0:T(8,128)(2,1)} %own.1), channel_id=1, source_target_pairs={{0,2},{1,3},{2,0},{3,1},{4,6},{5,7},{6,4},{7,5},{8,10},{9,11},{10,... | collective-permute-start | bytes 786440 | tf_op jit(solution)/shard_map/ppermute | solution.py:436
  18.9 8.9 %collective-permute-start = (bf16[128,512]{1,0:T(8,128)(2,1)}, bf16[128,512]{1,0:T(8,128)(2,1)S(1)}, u32[]{:S(2)}, u32[]{:S(2)}) collective-permute-start(bf16[128,512]{1,0:T(8,128)(2,1)} %get-tuple-element.65), channel_id=1, source_target_pairs={{0,4},{4,8},{8,12},{12,16},{16,20},{20,24},{24,28},{28,32},{32,36}... | collective-permute-start | bytes 393224 | tf_op jit(solution)/shard_map/ppermute | solution.py:475
  27.8 14.1 %copy-start.11 = (bf16[64,2048]{1,0:T(8,128)(2,1)}, bf16[64,2048]{1,0:T(8,128)(2,1)S(1)}, u32[]{:S(2)}) copy-start(bf16[64,2048]{1,0:T(8,128)(2,1)S(1)} %collective-permute-done.1.piece2) | copy-start | bytes 786436
  29.3 21.2 %all-to-all-start.1 = ((bf16[64,16,128]{2,1,0:T(8,128)(2,1)}), bf16[64,16,128]{2,1,0:T(8,128)(2,1)S(1)}, u32[]{:S(2)}, u32[]{:S(2)}) async-start(bf16[64,16,128]{2,1,0:T(8,128)(2,1)} %chain_fwd.1), calls=%async_computation.1 | async-start | bytes 524288 | tf_op jit(solution)/shard_map/all_to_all | solution.py:418
  38.0 8.6 %collective-permute-start.2 = (bf16[64,2048]{1,0:T(8,128)(2,1)}, bf16[64,2048]{1,0:T(8,128)(2,1)S(1)}, u32[]{:S(2)}, u32[]{:S(2)}) collective-permute-start(bf16[64,2048]{1,0:T(8,128)(2,1)} %own.1), channel_id=1, source_target_pairs={{0,1},{1,2},{2,3},{3,0},{4,5},{5,6},{6,7},{7,4},{8,9},{9,10},{10,1... | collective-permute-start | bytes 786440 | tf_op jit(solution)/shard_map/ppermute | solution.py:436
  39.6 8.3 %collective-permute-start.3 = (bf16[64,2048]{1,0:T(8,128)(2,1)}, bf16[64,2048]{1,0:T(8,128)(2,1)S(1)}, u32[]{:S(2)}, u32[]{:S(2)}) collective-permute-start(bf16[64,2048]{1,0:T(8,128)(2,1)} %own.1), channel_id=1, source_target_pairs={{0,3},{1,0},{2,1},{3,2},{4,7},{5,4},{6,5},{7,6},{8,11},{9,8},{10,9... | collective-permute-start | bytes 786440 | tf_op jit(solution)/shard_map/ppermute | solution.py:436
  46.3 4.2 %copy-start = (bf16[512,16]{1,0:T(8,128)(2,1)S(1)}, bf16[512,16]{1,0:T(8,128)(2,1)}, u32[]{:S(2)}) copy-start(bf16[512,16]{1,0:T(8,128)(2,1)} %constant.23.clone.sel) | copy-start | bytes 49156
  46.3 4.2 %copy-start.3 = (bf16[256,64]{0,1:T(8,128)(2,1)S(1)}, bf16[256,64]{0,1:T(8,128)(2,1)}, u32[]{:S(2)}) copy-start(bf16[256,64]{0,1:T(8,128)(2,1)} %param.17) | copy-start | bytes 98308
  46.3 4.2 %copy-start.6 = (f32[512]{0:T(512)S(1)}, f32[512]{0:T(512)}, u32[]{:S(2)}) copy-start(f32[512]{0:T(512)} %param.21) | copy-start | bytes 6148
  46.7 1.2 %copy-start.9 = (bf16[64,2048]{1,0:T(8,128)(2,1)}, bf16[64,2048]{1,0:T(8,128)(2,1)S(1)}, u32[]{:S(2)}) copy-start(bf16[64,2048]{1,0:T(8,128)(2,1)S(1)} %collective-permute-done.2.piece1) | copy-start | bytes 786436
  47.9 0.7 copy-start.10
  52.8 21.9 %all-to-all-start.2 = ((bf16[64,16,128]{2,1,0:T(8,128)(2,1)}), bf16[64,16,128]{2,1,0:T(8,128)(2,1)S(1)}, u32[]{:S(2)}, u32[]{:S(2)}) async-start(bf16[64,16,128]{2,1,0:T(8,128)(2,1)} %bitcast.22), calls=%async_computation.2 | async-start | bytes 524288 | tf_op jit(solution)/shard_map/all_to_all | solution.py:418
  66.3 27.7 %copy-start.8 = (bf16[64,2048]{1,0:T(8,128)(2,1)S(1)}, bf16[64,2048]{1,0:T(8,128)(2,1)}, u32[]{:S(2)}) copy-start(bf16[64,2048]{1,0:T(8,128)(2,1)} %get-tuple-element.100) | copy-start | bytes 786436
  66.3 27.7 %collective-permute-start.4 = (bf16[64,2048]{1,0:T(8,128)(2,1)}, bf16[64,2048]{1,0:T(8,128)(2,1)S(1)}, u32[]{:S(2)}, u32[]{:S(2)}) collective-permute-start(bf16[64,2048]{1,0:T(8,128)(2,1)} %get-tuple-element.101), channel_id=1, source_target_pairs={{0,1},{1,2},{2,3},{3,0},{4,5},{5,6},{6,7},{7,4},{8,9},{9,10},{10,1... | collective-permute-start | bytes 786440 | tf_op jit(solution)/shard_map/ppermute | solution.py:436
  67.6 26.4 %collective-permute-start.5 = (bf16[64,2048]{1,0:T(8,128)(2,1)}, bf16[64,2048]{1,0:T(8,128)(2,1)}, u32[]{:S(2)}, u32[]{:S(2)}) collective-permute-start(bf16[64,2048]{1,0:T(8,128)(2,1)} %get-tuple-element.102), channel_id=1, source_target_pairs={{0,2},{1,3},{2,0},{3,1},{4,6},{5,7},{6,4},{7,5},{8,10},{9,11},{10,... | collective-permute-start | bytes 786440 | tf_op jit(solution)/shard_map/ppermute | solution.py:436
  69.8 24.3 %collective-permute-start.6 = (bf16[64,2048]{1,0:T(8,128)(2,1)}, bf16[64,2048]{1,0:T(8,128)(2,1)}, u32[]{:S(2)}, u32[]{:S(2)}) collective-permute-start(bf16[64,2048]{1,0:T(8,128)(2,1)} %get-tuple-element.103), channel_id=1, source_target_pairs={{0,3},{1,0},{2,1},{3,2},{4,7},{5,4},{6,5},{7,6},{8,11},{9,8},{10,9... | collective-permute-start | bytes 786440 | tf_op jit(solution)/shard_map/ppermute | solution.py:436
  75.5 24.0 %all-to-all-start.3 = ((bf16[64,16,128]{2,1,0:T(8,128)(2,1)}), bf16[64,16,128]{2,1,0:T(8,128)(2,1)S(1)}, u32[]{:S(2)}, u32[]{:S(2)}) async-start(bf16[64,16,128]{2,1,0:T(8,128)(2,1)} %chain_back.1), calls=%async_computation.3 | async-start | bytes 524288 | tf_op jit(solution)/shard_map/all_to_all | solution.py:418
  87.1 12.4 %copy-start.1 = (bf16[512,16]{1,0:T(8,128)(2,1)S(1)}, bf16[512,16]{1,0:T(8,128)(2,1)}, u32[]{:S(2)}) copy-start(bf16[512,16]{1,0:T(8,128)(2,1)} %constant.21.clone.sel) | copy-start | bytes 49156
  87.1 12.4 %copy-start.2 = (bf16[256,64]{0,1:T(8,128)(2,1)S(1)}, bf16[256,64]{0,1:T(8,128)(2,1)}, u32[]{:S(2)}) copy-start(bf16[256,64]{0,1:T(8,128)(2,1)} %param.18) | copy-start | bytes 98308
  87.1 12.4 %copy-start.4 = (bf16[256,512]{1,0:T(8,128)(2,1)S(1)}, bf16[256,512]{1,0:T(8,128)(2,1)}, u32[]{:S(2)}) copy-start(bf16[256,512]{1,0:T(8,128)(2,1)} %get-tuple-element.111.faded) | copy-start | bytes 786436
  87.1 12.4 %copy-start.5 = (bf16[16,512]{1,0:T(8,128)(2,1)S(1)}, bf16[16,512]{1,0:T(8,128)(2,1)}, u32[]{:S(2)}) copy-start(bf16[16,512]{1,0:T(8,128)(2,1)} %constant.22.clone.sel_kt.sel_t) | copy-start | bytes 49156
  89.4 10.1 %collective-permute-start.7 = (bf16[128,512]{1,0:T(8,128)(2,1)}, bf16[128,512]{1,0:T(8,128)(2,1)S(1)}, u32[]{:S(2)}, u32[]{:S(2)}) collective-permute-start(bf16[128,512]{1,0:T(8,128)(2,1)} %edge_grad.1), channel_id=1, source_target_pairs={{4,0},{8,4},{12,8},{16,12},{20,16},{24,20},{28,24},{32,28},{36,32}... | collective-permute-start | bytes 393224 | tf_op jit(solution)/shard_map/ppermute | solution.py:552
